TPU v7x, 1024 devices: a whole 8x8x8 slice. The times are simulated.
1024 devices in a mesh: tile: 128 (over z, x, core), lev: 8 (over y).
Axes of the slice: x: 8, y: 8, z: 8, core: 2. Of those that a mesh axis runs over, the one named last changes fastest.
Arguments:
- theta: float32 [128, 32, 16384], P('lev', None, 'tile'), may hold values from -6 to 6
- thickness: float32 [128, 32, 16384], P('lev', None, 'tile'), may hold values from 0.5 to 1.5
- wind: float32 [128, 32, 16384], P('lev', None, 'tile'), may hold values from -6 to 6
- surface: float32 [32, 16384], P(None, 'tile'), may hold values from -6 to 6
- trigger: int32 [32, 16384], P(None, 'tile'), may hold values 0 or 1
- closure: int32 [32, 16384], P(None, 'tile'), may hold values from 0 to 2
- closure_weights: bfloat16 [4, 128, 128], replicated, may hold values from -0.5 to 0.5
Outputs:
- pressure: float32 [128, 32, 16384], P('lev', None, 'tile')
- wind_next: float32 [128, 32, 16384], P('lev', None, 'tile')
- heating: bfloat16 [128, 32, 16384], P('lev', None, 'tile')
Inputs may be any that keep to these rules, and one draw needn't show every extreme that they name: trigger[r, c] is 0 or 1 in every draw. closure[r, c] is one of 0 .. 2 in every draw.
All inputs are finite; a program needn't handle non-finite values. No bound on the sum of `trigger` on one device may be relied on, other than what follows from the above.
Results may differ from a plain program's by a relative error of at most 0.0049.
Values may be sent and summed in bfloat16 or wider, within the bound.
No kernel may reach another device: no remote copies, remote signals or barrier semaphores. Data moves between devices by JAX's collectives and lax.ppermute only.
A program may use at most 32 MiB of HBM per device.

v0:
```python
import jax
import jax.numpy as jnp
from jax import lax
from jax.sharding import PartitionSpec as P

LEVELS = 128
SUBSTEPS = 6


courant = 0.9


def copy_for_each(array, axis):
    size = lax.axis_size(axis)
    return lax.all_to_all(
        jnp.broadcast_to(array[None], (size, *array.shape)), axis, 0, 0, tiled=True
    )


def folded_in_pairs(pieces, combine):
    while len(jax.tree.leaves(pieces)[0]) > 1:
        pieces = jax.vmap(combine)(*(pieces[side::2] for side in (0, 1)))
    return pieces[0]


def carried_in(array, axis, combine, identity):
    size, position = (lax.axis_size(axis), lax.axis_index(axis))
    passed = jnp.arange(size) > position

    def kept(part, zero, own):
        part = jnp.where(
            passed.reshape(-1, *(1 for _ in own.shape)), part, jnp.asarray(zero, own.dtype)
        )
        return part[::-1]

    pieces = copy_for_each(array, axis)
    return folded_in_pairs(kept(pieces, identity, array), combine)


def with_halo(cells, sides, width):
    for axis, dim in sides:
        count = lax.axis_size(axis)
        head = lax.slice_in_dim(cells, 0, width, axis=dim)
        tail = lax.slice_in_dim(cells, cells.shape[dim] - width, cells.shape[dim], axis=dim)
        cells = jnp.concatenate(
            [
                lax.ppermute(tail, axis, [(i, (i + 1) % count) for i in range(count)]),
                cells,
                lax.ppermute(head, axis, [((i + 1) % count, i) for i in range(count)]),
            ],
            axis=dim,
        )
    return cells


def add_pair(earlier, later):
    return earlier + later


def advance(extended):
    pressure = extended[0]
    velocity = extended[1]
    velocity = velocity[:, :, :-1] - courant * (pressure[:, :, 1:] - pressure[:, :, :-1])
    pressure = pressure[:, :, 1:-1] - courant * (velocity[:, :, 1:] - velocity[:, :, :-1])
    return jnp.stack([pressure, velocity[:, :, 1:]])


def combine_heating(products, triggers_here, closures_here):
    schemes = products.shape[0] - 1
    onehot = (
        closures_here[None, :, :] == jnp.arange(schemes, dtype=jnp.int32)[:, None, None]
    ).astype(jnp.float32)
    convect = jnp.sum(products[:schemes] * onehot[:, None, :, :], axis=0)
    return products[schemes] + triggers_here.astype(jnp.float32)[None, :, :] * convect


def shards(theta, thickness, wind, surface, trigger, closure, closure_weights):
    row_count = theta.shape[1]
    longitudes = theta.shape[2]
    lev_count = lax.axis_size("lev")
    lev_rank = lax.axis_index("lev")
    thermal = theta * thickness * LEVELS ** (-0.5)
    column_total = jnp.sum(thermal, axis=0)
    higher = carried_in(column_total, "lev", add_pair, jnp.zeros_like(column_total))
    suffix = lax.cumsum(thermal, axis=0, reverse=True) - thermal
    geopot = surface[None, :, :] + higher[None, :, :] + suffix + 0.5 * thermal
    fields = jnp.stack([geopot, wind])
    extended = with_halo(fields, (("tile", 3),), SUBSTEPS)
    for substep in range(SUBSTEPS):
        extended = advance(extended)
    fields = extended
    local_theta = theta.astype(jnp.bfloat16)
    portion = longitudes // lev_count
    whole_columns = lax.all_to_all(local_theta, "lev", split_axis=2, concat_axis=0, tiled=True)
    triggers_here = lax.dynamic_slice_in_dim(trigger, lev_rank * portion, portion, 1)
    closures_here = lax.dynamic_slice_in_dim(closure, lev_rank * portion, portion, 1)
    stacked = closure_weights.reshape(
        (closure_weights.shape[0] * closure_weights.shape[1], closure_weights.shape[2])
    )
    flat_columns = whole_columns.reshape((whole_columns.shape[0], row_count * portion))
    products = jnp.dot(stacked, flat_columns, preferred_element_type=jnp.float32)
    products = products.reshape(
        (closure_weights.shape[0], closure_weights.shape[1], row_count, portion)
    )
    heat_cols = combine_heating(products, triggers_here, closures_here).astype(jnp.bfloat16)
    heating = lax.all_to_all(heat_cols, "lev", split_axis=0, concat_axis=2, tiled=True)
    return (fields[0], fields[1], heating)


def solution(mesh):
    in_specs = (
        P("lev", None, "tile"),
        P("lev", None, "tile"),
        P("lev", None, "tile"),
        P(None, "tile"),
        P(None, "tile"),
        P(None, "tile"),
        P(),
    )
    out_specs = (P("lev", None, "tile"), P("lev", None, "tile"), P("lev", None, "tile"))
    return jax.shard_map(shards, mesh=mesh, in_specs=in_specs, out_specs=out_specs, check_vma=False)
```

profile of v0, /device:TPU:16, one launch (start us, length us, event | category | flops | bytes accessed | tf_op | source)
XLA Modules:
  0.0 73.3 jit_solution(6370579850212619785)
XLA Ops:
  0.6 1.2 %fusion.34 = (bf16[16,32,128]{2,1,0:T(8,128)(2,1)S(1)}, f32[32,128]{1,0:T(8,128)S(1)}) fusion(f32[16,32,128]{2,1,0:T(8,128)} %param.7, f32[16,32,128]{2,1,0:T(8,128)} %param.8), kind=kLoop, calls=%fused_computation.63 | loop fusion | flops 258048 | bytes 671744 | tf_op jit(solution)/shard_map/convert_element_type | solution.py:92
  1.9 0.4 copy.36
  2.3 1.2 %reshape.31 = bf16[8,2,4096]{2,1,0:T(2,128)(2,1)} reshape(bf16[128,16,32]{2,1,0:T(8,128)(2,1)S(1)} %bitcast.33) | data formatting | bytes 262144
  3.5 16.4 %all-to-all-start.1 = ((bf16[8,2,4096]{2,1,0:T(2,128)(2,1)}), bf16[8,2,4096]{2,1,0:T(2,128)(2,1)S(1)}, u32[]{:S(2)}, u32[]{:S(2)}) async-start(bf16[8,2,4096]{2,1,0:T(2,128)(2,1)} %reshape.31), calls=%async_computation.1 | async-start | bytes 262144 | tf_op jit(solution)/shard_map/all_to_all | solution.py:94
  20.1 7.4 %all-to-all-done.1 = bf16[8,2,4096]{2,1,0:T(2,128)(2,1)S(1)} async-done(((bf16[8,2,4096]{2,1,0:T(2,128)(2,1)}), bf16[8,2,4096]{2,1,0:T(2,128)(2,1)S(1)}, u32[]{:S(2)}, u32[]{:S(2)}) %all-to-all-start.1) | async-done | bytes 131104 | tf_op jit(solution)/shard_map/all_to_all | solution.py:94
  27.5 0.7 broadcast_in_dim.28
  28.1 4.8 %all-to-all-start = ((f32[8,32,128]{2,1,0:T(8,128)}), f32[8,32,128]{2,1,0:T(8,128)S(1)}, u32[]{:S(2)}, u32[]{:S(2)}) async-start(f32[8,32,128]{2,1,0:T(8,128)} %broadcast_in_dim.28), calls=%async_computation | async-start | bytes 262144 | tf_op jit(solution)/shard_map/all_to_all | solution.py:15
  33.2 0.6 copy.38
  33.8 1.8 %reshape.30 = bf16[128,512]{1,0:T(8,128)(2,1)S(1)} reshape(bf16[8,16,32,16]{3,2,1,0:T(8,128)(2,1)S(1)} %copy.38) | data formatting | bytes 262144 | tf_op jit(solution)/shard_map/reshape | solution.py:100
  35.6 0.3 fusion.36
  35.9 1.0 %copy-done.1 = f32[512,512]{0,1:T(8,128)} copy-done((f32[512,512]{0,1:T(8,128)}, f32[512,512]{0,1:T(8,128)S(1)}, u32[]{:S(2)}) %copy-start.1) | copy-done | bytes 1048600
  36.9 3.7 %all-to-all-done = f32[8,32,128]{2,1,0:T(8,128)S(1)} async-done(((f32[8,32,128]{2,1,0:T(8,128)}), f32[8,32,128]{2,1,0:T(8,128)S(1)}, u32[]{:S(2)}, u32[]{:S(2)}) %all-to-all-start) | async-done | bytes 131104 | tf_op jit(solution)/shard_map/all_to_all | solution.py:15
  40.8 0.7 %copy-done.7 = f32[32,128]{1,0:T(8,128)S(1)} copy-done((f32[32,128]{1,0:T(8,128)S(1)}, f32[32,128]{1,0:T(8,128)}, u32[]{:S(2)}) %copy-start.7) | copy-done | bytes 16408
  41.9 0.8 %copy-done.4 = f32[16,32,128]{2,1,0:T(8,128)S(1)} copy-done((f32[16,32,128]{2,1,0:T(8,128)S(1)}, f32[16,32,128]{2,1,0:T(8,128)}, u32[]{:S(2)}) %copy-start.4) | copy-done | bytes 262168
  42.7 1.2 %slice_maximum_fusion = (f32[2,16,32,6]{3,2,1,0:T(8,128)}, f32[2,16,32,6]{3,2,1,0:T(8,128)}) fusion(f32[1,16,32,128]{3,2,1,0:T(8,128)S(1)} %bitcast.37, f32[1,16,32,128]{3,2,1,0:T(8,128)S(1)} %fusion.2), kind=kLoop, calls=%fused_computation.42 | loop fusion | flops 12288 | bytes 573440 | tf_op jit(solution)/shard_map/stack | solution.py:87
  43.9 7.8 %collective-permute-start.1 = (f32[2,16,32,6]{3,2,1,0:T(8,128)}, f32[2,16,32,6]{3,2,1,0:T(8,128)S(1)}, u32[]{:S(2)}, u32[]{:S(2)}) collective-permute-start(f32[2,16,32,6]{3,2,1,0:T(8,128)} %get-tuple-element.23), channel_id=1, source_target_pairs={{8,0},{16,8},{24,16},{32,24},{40,32},{48,40},{56,48},{64,56},{72,6... | collective-permute-start | bytes 73736 | tf_op jit(solution)/shard_map/ppermute | solution.py:49
  51.7 1.9 %collective-permute-start = (f32[2,16,32,6]{3,2,1,0:T(8,128)}, f32[2,16,32,6]{3,2,1,0:T(8,128)}, u32[]{:S(2)}, u32[]{:S(2)}) collective-permute-start(f32[2,16,32,6]{3,2,1,0:T(8,128)} %get-tuple-element.22), channel_id=1, source_target_pairs={{0,8},{8,16},{16,24},{24,32},{32,40},{40,48},{48,56},{56,64},{64,7... | collective-permute-start | bytes 73736 | tf_op jit(solution)/shard_map/ppermute | solution.py:47
  54.0 0.8 %multiply_reduce_fusion = f32[128,32,16]{0,2,1:T(8,128)S(1)} fusion(f32[3,128,32,16]{1,0,3,2:T(4,128)S(1)} %slice.217, f32[3,32,16]{0,2,1:T(8,128)S(1)} %fusion.27), kind=kLoop, calls=%fused_computation.5 | loop fusion | flops 327680 | bytes 1054720 | tf_op jit(solution)/shard_map/reduce_sum | solution.py:73
  55.1 0.5 copy.39
  55.6 1.2 %reshape.33 = bf16[8,2,4096]{2,1,0:T(2,128)(2,1)} reshape(bf16[128,16,32]{2,1,0:T(8,128)(2,1)S(1)} %bitcast.34) | data formatting | bytes 262144
  56.7 4.8 %all-to-all-start.2 = ((bf16[8,2,4096]{2,1,0:T(2,128)(2,1)}), bf16[8,2,4096]{2,1,0:T(2,128)(2,1)S(1)}, u32[]{:S(2)}, u32[]{:S(2)}) async-start(bf16[8,2,4096]{2,1,0:T(2,128)(2,1)} %reshape.33), calls=%async_computation.2 | async-start | bytes 262144 | tf_op jit(solution)/shard_map/all_to_all | solution.py:106
  61.6 4.3 %collective-permute-done = f32[2,16,32,6]{3,2,1,0:T(8,128)} collective-permute-done((f32[2,16,32,6]{3,2,1,0:T(8,128)}, f32[2,16,32,6]{3,2,1,0:T(8,128)}, u32[]{:S(2)}, u32[]{:S(2)}) %collective-permute-start) | collective-permute-done | bytes 24608 | tf_op jit(solution)/shard_map/ppermute | solution.py:47
  65.9 1.5 %pad_maximum_fusion = f32[2,16,32,140]{3,2,1,0:T(8,128)S(1)} fusion(f32[2,16,32,6]{3,2,1,0:T(8,128)S(1)} %collective-permute-done.1, f32[1,16,32,128]{3,2,1,0:T(8,128)S(1)} %bitcast.38, f32[1,16,32,128]{3,2,1,0:T(8,128)S(1)} %fusion.2, f32[2,16,32,6]{3,2,1,0:T(8,128)} %collective-permute-done), kind=kLoop, calls=%fused_computation.4 | loop fusion | flops 430080 | bytes 1146880 | tf_op jit(solution)/shard_map/concatenate | solution.py:45
  67.7 0.3 fusion.22
  68.0 0.3 fusion.20
  68.4 0.3 fusion.18
  68.7 0.3 fusion.16
  69.1 0.3 fusion.14
  69.4 0.3 fusion.12
  69.7 0.3 fusion.10
  71.1 1.0 %fusion.26 = (f32[16,32,128]{2,1,0:T(8,128)}, f32[16,32,128]{2,1,0:T(8,128)}) fusion(f32[16,32,129]{2,1,0:T(8,128)S(1)} %fusion.4, f32[16,32,130]{2,1,0:T(8,128)S(1)} %fusion.6), kind=kLoop, calls=%fused_computation.45 | loop fusion | flops 196608 | bytes 1310720 | tf_op jit(solution)/shard_map/sub | solution.py:64
  72.4 0.8 %copy.41 = bf16[16,32,128]{2,1,0:T(8,128)(2,1)} copy(bf16[16,32,128]{1,2,0:T(8,128)(2,1)S(1)} %bitcast.36) | data formatting | bytes 262144
  (38 shorter events, 3.1 us)
Async XLA Ops:
  0.6 34.9 %copy-start = (bf16[4,128,128]{2,1,0:T(8,128)(2,1)S(1)}, bf16[4,128,128]{2,1,0:T(8,128)(2,1)}, u32[]{:S(2)}) copy-start(bf16[4,128,128]{2,1,0:T(8,128)(2,1)} %param.13) | copy-start | bytes 393220
  3.5 16.4 %copy-start.5 = (s32[32,128]{1,0:T(8,128)S(1)}, s32[32,128]{1,0:T(8,128)}, u32[]{:S(2)}) copy-start(s32[32,128]{1,0:T(8,128)} %param.11) | copy-start | bytes 49156
  3.5 16.4 %copy-start.6 = (s32[32,128]{1,0:T(8,128)S(1)}, s32[32,128]{1,0:T(8,128)}, u32[]{:S(2)}) copy-start(s32[32,128]{1,0:T(8,128)} %param.12) | copy-start | bytes 49156
  3.5 24.0 %all-to-all-start.1 = ((bf16[8,2,4096]{2,1,0:T(2,128)(2,1)}), bf16[8,2,4096]{2,1,0:T(2,128)(2,1)S(1)}, u32[]{:S(2)}, u32[]{:S(2)}) async-start(bf16[8,2,4096]{2,1,0:T(2,128)(2,1)} %reshape.31), calls=%async_computation.1 | async-start | bytes 262144 | tf_op jit(solution)/shard_map/all_to_all | solution.py:94
  28.1 12.5 %all-to-all-start = ((f32[8,32,128]{2,1,0:T(8,128)}), f32[8,32,128]{2,1,0:T(8,128)S(1)}, u32[]{:S(2)}, u32[]{:S(2)}) async-start(f32[8,32,128]{2,1,0:T(8,128)} %broadcast_in_dim.28), calls=%async_computation | async-start | bytes 262144 | tf_op jit(solution)/shard_map/all_to_all | solution.py:15
  35.9 1.0 %copy-start.1 = (f32[512,512]{0,1:T(8,128)}, f32[512,512]{0,1:T(8,128)S(1)}, u32[]{:S(2)}) copy-start(f32[512,512]{0,1:T(8,128)S(1)} %fusion.36) | copy-start | bytes 3145732
  40.7 1.0 %copy-start.2 = (f32[16,32,128]{2,1,0:T(8,128)S(1)}, f32[16,32,128]{2,1,0:T(8,128)}, u32[]{:S(2)}) copy-start(f32[16,32,128]{2,1,0:T(8,128)} %param.7) | copy-start | bytes 786436
  40.7 1.0 %copy-start.3 = (f32[16,32,128]{2,1,0:T(8,128)S(1)}, f32[16,32,128]{2,1,0:T(8,128)}, u32[]{:S(2)}) copy-start(f32[16,32,128]{2,1,0:T(8,128)} %param.8) | copy-start | bytes 786436
  40.8 0.8 %copy-start.7 = (f32[32,128]{1,0:T(8,128)S(1)}, f32[32,128]{1,0:T(8,128)}, u32[]{:S(2)}) copy-start(f32[32,128]{1,0:T(8,128)} %param.10) | copy-start | bytes 49156
  41.8 0.9 %copy-start.4 = (f32[16,32,128]{2,1,0:T(8,128)S(1)}, f32[16,32,128]{2,1,0:T(8,128)}, u32[]{:S(2)}) copy-start(f32[16,32,128]{2,1,0:T(8,128)} %param.9) | copy-start | bytes 786436
  42.7 11.0 %slice-start.1 = ((f32[512,512]{0,1:T(8,128)}), f32[384,512]{0,1:T(8,128)S(1)}, s32[]{:S(2)}) async-start(f32[512,512]{0,1:T(8,128)} %copy-done.1), calls=%async_computation.4 | async-start | bytes 1572864 | tf_op jit(solution)/shard_map/slice | solution.py:73
  43.9 17.7 %collective-permute-start.1 = (f32[2,16,32,6]{3,2,1,0:T(8,128)}, f32[2,16,32,6]{3,2,1,0:T(8,128)S(1)}, u32[]{:S(2)}, u32[]{:S(2)}) collective-permute-start(f32[2,16,32,6]{3,2,1,0:T(8,128)} %get-tuple-element.23), channel_id=1, source_target_pairs={{8,0},{16,8},{24,16},{32,24},{40,32},{48,40},{56,48},{64,56},{72,6... | collective-permute-start | bytes 73736 | tf_op jit(solution)/shard_map/ppermute | solution.py:49
  51.7 14.1 %collective-permute-start = (f32[2,16,32,6]{3,2,1,0:T(8,128)}, f32[2,16,32,6]{3,2,1,0:T(8,128)}, u32[]{:S(2)}, u32[]{:S(2)}) collective-permute-start(f32[2,16,32,6]{3,2,1,0:T(8,128)} %get-tuple-element.22), channel_id=1, source_target_pairs={{0,8},{8,16},{16,24},{24,32},{32,40},{40,48},{48,56},{56,64},{64,7... | collective-permute-start | bytes 73736 | tf_op jit(solution)/shard_map/ppermute | solution.py:47
  54.0 1.0 %slice-start = ((f32[512,512]{0,1:T(8,128)}), f32[128,512]{0,1:T(8,128)S(1)}, s32[]{:S(2)}) async-start(f32[512,512]{0,1:T(8,128)} %copy-done.1), calls=%async_computation.3 | async-start | bytes 524288 | tf_op jit(solution)/shard_map/slice | solution.py:74
  56.7 15.3 %all-to-all-start.2 = ((bf16[8,2,4096]{2,1,0:T(2,128)(2,1)}), bf16[8,2,4096]{2,1,0:T(2,128)(2,1)S(1)}, u32[]{:S(2)}, u32[]{:S(2)}) async-start(bf16[8,2,4096]{2,1,0:T(2,128)(2,1)} %reshape.33), calls=%async_computation.2 | async-start | bytes 262144 | tf_op jit(solution)/shard_map/all_to_all | solution.py:106
where the time goes:
time: 73.9 us; the launch traced here: 73.3 us
  starting transfers between devices  35.8 us (48%)
  waiting for transfers between devices  15.4 us (21%)
  local copies, waits for them, and re-layouts  10.9 us (15%)
  other arithmetic  9.87 us (13%)
  between operations  0.91 us (1%)
    all_to_all x1, starting transfers between devices, shards(): lax.all_to_all(local_theta, 'lev', split_axis=2, concat_axis=0, tiled=True)  16.4 us
    ppermute x1, starting transfers between devices, with_halo(): lax.ppermute(head, axis, [((i + 1) % count, i) for i in range(count)])  7.83 us
    all_to_all x1, waiting for transfers between devices, shards(): lax.all_to_all(local_theta, 'lev', split_axis=2, concat_axis=0, tiled=True)  7.41 us
    unnamed x21, local copies, waits for them, and re-layouts  6.48 us
    all_to_all x1, starting transfers between devices, copy_for_each(): lax.all_to_all(jnp.broadcast_to(array[None], (size, *array.shape)), axis,...  4.83 us
    all_to_all x1, starting transfers between devices, shards(): lax.all_to_all(heat_cols, 'lev', split_axis=0, concat_axis=2, tiled=True)  4.81 us
    ppermute x1, waiting for transfers between devices, with_halo(): lax.ppermute(tail, axis, [(i, (i + 1) % count) for i in range(count)])  4.32 us
    all_to_all x1, waiting for transfers between devices, copy_for_each(): lax.all_to_all(jnp.broadcast_to(array[None], (size, *array.shape)), axis,...  3.7 us
  transfers between devices with their start and end apart: 5, of which 3 were waited for; matrix products, arithmetic and copies ran while one was open for 17% of the time, Pallas kernels for 0%

commit v1 on v0

v1 whole, which is shorter than its diff:
```python
import jax
import jax.numpy as jnp
from jax import lax
from jax.experimental import pallas as pl
from jax.experimental.pallas import tpu as pltpu
from jax.sharding import PartitionSpec as P

LEVELS = 128
SUBSTEPS = 6
COURANT = 0.9
SCALE = LEVELS ** (-0.5)
PEERS = 8
OWN = 16
ROWS = 32
LANES = 128
BAND = 4
FIRST = 80
SECOND = 96
BF16 = jnp.bfloat16
F32 = jnp.float32


def lanes_of(shape):
    return lax.broadcasted_iota(jnp.int32, shape, len(shape) - 1)


def rows_of(shape):
    return lax.broadcasted_iota(jnp.int32, shape, len(shape) - 2)


def turned(x, shift):
    return pltpu.roll(x, shift % LANES, 1)


def halves_swapped(x):
    return pltpu.roll(x, 4, 0)


def three_parts(x):
    high = x.astype(BF16).astype(F32)
    rest = x - high
    middle = rest.astype(BF16).astype(F32)
    return high, middle, rest - middle


def sub(a, b):
    return a - COURANT * b


def substeps(pressure, wind):
    for _ in range(SUBSTEPS):
        wind = sub(wind, turned(pressure, -1) - pressure)
        pressure = sub(pressure, wind - turned(wind, 1))
    return pressure, wind


def windowed(main, left, right):
    lane = lanes_of(main.shape)
    return jnp.where(
        lane < 6,
        left,
        jnp.where(lane < 32, turned(main, 6), jnp.where(lane < 76, turned(main, 76), right)),
    )


def edges_in(main, window):
    lane = lanes_of(main.shape)
    return jnp.where(
        lane < 6, turned(window, -6), jnp.where(lane >= 122, turned(window, 52), main)
    )


def send_columns(theta, thickness, out):
    total = jnp.zeros((ROWS, LANES), F32)
    for level in range(OWN):
        at = pl.ds(level * ROWS, ROWS)
        total = total + theta[at, :] * thickness[at, :] * SCALE
    for row in range(ROWS):
        picked = theta[pl.ds(row, OWN, stride=ROWS), :]
        out[row // BAND, pl.ds(OWN * (row % BAND), OWN), :] = picked.astype(BF16)
    top = rows_of((8, LANES)) < 4
    for group in range(4):
        high, middle, low = three_parts(total[8 * group : 8 * group + 8])
        first = jnp.where(top, high, halves_swapped(middle))
        second = jnp.where(top, halves_swapped(high), middle)
        out[2 * group, 64:80, :] = jnp.concatenate([first, jnp.where(top, low, 0.0)]).astype(BF16)
        out[2 * group + 1, 64:80, :] = jnp.concatenate(
            [second, jnp.where(top, halves_swapped(low), 0.0)]
        ).astype(BF16)


def send_borders(theta, thickness, wind, surface, to_right, to_left):
    lane = lanes_of((ROWS, LANES))
    zero = jnp.zeros((ROWS, LANES), F32)
    below = zero
    packed = [[zero, zero], [zero, zero]]
    for level in reversed(range(OWN)):
        at = pl.ds(level * ROWS, ROWS)
        thermal = theta[at, :] * thickness[at, :] * SCALE
        fields = (below + 0.5 * thermal, wind[at, :])
        below = below + thermal
        here = (lane >= 8 * level) & (lane < 8 * level + 8)
        for index, field in enumerate(fields):
            packed[0][index] = jnp.where(here, turned(field, 8 * level - 122), packed[0][index])
            packed[1][index] = jnp.where(here, turned(field, 8 * level), packed[1][index])
    ground = surface[...]
    for out, side, lead, first in ((to_right, 0, 0, 122), (to_left, 1, 8, 0)):
        out[0:32, :] = packed[side][0]
        out[32:64, :] = packed[side][1]
        sums = jnp.where((lane >= lead) & (lane < lead + 6), turned(below, lead - first), 0.0)
        out[64:96, :] = jnp.where(
            (lane >= lead + 16) & (lane < lead + 22), turned(ground, lead + 16 - first), sums
        )


def send_heating(got, trigger, closure, weights, from_left, from_right, out, stacked):
    lane = lanes_of((ROWS, LANES))
    me = lax.axis_index("lev")
    flags = trigger[pl.ds(BAND * me, BAND), :].astype(F32)
    scheme = closure[pl.ds(BAND * me, BAND), :]
    for row in range(BAND):
        chosen = [
            jnp.broadcast_to(
                jnp.where(scheme[row : row + 1] == s, flags[row : row + 1], 0.0), (OWN, LANES)
            ).astype(BF16)
            for s in range(3)
        ]
        columns = pl.ds(LANES * row, LANES)
        for peer in range(PEERS):
            block = got[peer, pl.ds(OWN * row, OWN), :]
            for s in range(3):
                stacked[pl.ds(LEVELS * s + OWN * peer, OWN), columns] = block * chosen[s]
            stacked[pl.ds(LEVELS * 3 + OWN * peer, OWN), columns] = block
    wide = jnp.concatenate([weights[s] for s in range(4)], axis=1)
    answer = jnp.dot(wide, stacked[...], preferred_element_type=F32).astype(BF16)
    for peer in range(PEERS):
        for row in range(BAND):
            out[peer, pl.ds(OWN * row, OWN), :] = answer[
                OWN * peer : OWN * peer + OWN, LANES * row : LANES * row + LANES
            ]
    borders = from_left[64:96, :] + from_right[64:96, :]
    borders = jnp.where(lane < 16, borders, 0.0)
    folded = borders[0:8]
    for group in range(1, 4):
        folded = folded + turned(borders[8 * group : 8 * group + 8], 32 * group)
    top = rows_of((8, LANES)) < 4
    bottom = halves_swapped(folded) + turned(folded, 16)
    higher = jnp.zeros((8, LANES), F32)
    for peer in reversed(range(PEERS)):
        high, middle, low = three_parts(jnp.where(top, higher, bottom))
        out[peer, 64:80, :] = jnp.concatenate([high, middle]).astype(BF16)
        out[peer, 80:96, :] = jnp.concatenate([low, jnp.zeros_like(low)]).astype(BF16)
        parts = got[peer, 64:80, :].astype(F32)
        higher = higher + ((parts[0:8] + halves_swapped(parts[0:8])) + parts[8:16])


def local_substeps(
    theta, thickness, wind, surface, from_left, from_right, out_p, out_w, main_p, main_w, side_p, side_w
):
    ground = surface[...]
    left_ground = turned(from_left[64:96, :], -16)
    right_ground = turned(from_right[64:96, :], 76 - 24)
    below = jnp.zeros((ROWS, LANES), F32)
    for level in reversed(range(OWN)):
        at = pl.ds(level * ROWS, ROWS)
        thermal = theta[at, :] * thickness[at, :] * SCALE
        p = ground + (below + 0.5 * thermal)
        below = below + thermal
        main_p[at, :] = p
        side_p[at, :] = windowed(
            p,
            turned(from_left[0:32, :], -8 * level) + left_ground,
            turned(from_right[0:32, :], 76 - 8 * level) + right_ground,
        )
        side_w[at, :] = windowed(
            wind[at, :],
            turned(from_left[32:64, :], -8 * level),
            turned(from_right[32:64, :], 76 - 8 * level),
        )
    p, w = substeps(main_p[...], wind[...])
    main_p[...] = p
    main_w[...] = w
    p, w = substeps(side_p[...], side_w[...])
    out_p[...] = edges_in(main_p[...], p)
    out_w[...] = edges_in(main_w[...], w)


def finish(got, local_p, local_w, out_p, out_w, out_h, rows_first):
    me = lax.axis_index("lev")
    top = rows_of((8, LANES)) < 4
    beyond = jnp.zeros((8, LANES), F32)
    pieces = []
    for peer in range(PEERS):
        tail = got[peer, 64:96, :].astype(F32)
        piece = (tail[0:8] + tail[8:16]) + tail[16:24]
        pieces.append(piece)
        beyond = beyond + jnp.where(me < peer, 1.0, 0.0) * piece
    unfolded = jnp.where(top, halves_swapped(beyond), turned(beyond, -16))
    main = jnp.concatenate(
        [
            jnp.where(top, pieces[2 * group], halves_swapped(pieces[2 * group + 1]))
            for group in range(4)
        ]
    )
    border = jnp.concatenate([turned(unfolded, -32 * group) for group in range(4)])
    side = windowed(main, border, turned(border, 76 - 8))
    zero = jnp.zeros((ROWS, LANES), F32)
    add_p, add_w = substeps(main, zero)
    side_p, side_w = substeps(side, zero)
    add_p = edges_in(add_p, side_p)
    add_w = edges_in(add_w, side_w)
    for level in range(OWN):
        at = pl.ds(level * ROWS, ROWS)
        out_p[at, :] = local_p[at, :] + add_p
        out_w[at, :] = local_w[at, :] + add_w
    for peer in range(PEERS):
        rows_first[pl.ds(64 * peer, 64), :] = got[peer, 0:64, :].astype(F32)
    for level in range(OWN):
        out_h[pl.ds(level * ROWS, ROWS), :] = rows_first[pl.ds(level, ROWS, stride=OWN), :].astype(
            BF16
        )


def call(kernel, outs, scratch=(), flops=100000, moved=1000000, room=8 << 20):
    return pl.pallas_call(
        kernel,
        out_shape=tuple(jax.ShapeDtypeStruct(s, d) for s, d in outs),
        scratch_shapes=[pltpu.VMEM(s, d) for s, d in scratch],
        compiler_params=pltpu.CompilerParams(vmem_limit_bytes=room),
        cost_estimate=pl.CostEstimate(flops=flops, bytes_accessed=moved, transcendentals=0),
    )


def shards(theta, thickness, wind, surface, trigger, closure, closure_weights):
    flat = (OWN * ROWS, LANES)
    theta, thickness, wind = (x.reshape(flat) for x in (theta, thickness, wind))
    tiles = lax.axis_size("tile")
    (columns,) = call(send_columns, [((PEERS, FIRST, LANES), BF16)], room=60 << 20)(theta, thickness)
    columns = lax.all_to_all(columns, "lev", 0, 0, tiled=True)
    to_right, to_left = call(send_borders, [((96, LANES), F32)] * 2)(
        theta, thickness, wind, surface
    )
    from_left = lax.ppermute(to_right, "tile", [(i, (i + 1) % tiles) for i in range(tiles)])
    from_right = lax.ppermute(to_left, "tile", [((i + 1) % tiles, i) for i in range(tiles)])
    (heats,) = call(
        send_heating, [((PEERS, SECOND, LANES), BF16)], [((512, 512), BF16)], flops=70000000
    )(columns, trigger, closure, closure_weights, from_left, from_right)
    heats = lax.all_to_all(heats, "lev", 0, 0, tiled=True)
    local_p, local_w = call(local_substeps, [(flat, F32)] * 2, [(flat, F32)] * 4, flops=20000000)(
        theta, thickness, wind, surface, from_left, from_right
    )
    pressure, wind_next, heating = call(
        finish, [(flat, F32), (flat, F32), (flat, BF16)], [(flat, F32)]
    )(heats, local_p, local_w)
    shape = (OWN, ROWS, LANES)
    return pressure.reshape(shape), wind_next.reshape(shape), heating.reshape(shape)


def solution(mesh):
    in_specs = (
        P("lev", None, "tile"),
        P("lev", None, "tile"),
        P("lev", None, "tile"),
        P(None, "tile"),
        P(None, "tile"),
        P(None, "tile"),
        P(),
    )
    out_specs = (P("lev", None, "tile"), P("lev", None, "tile"), P("lev", None, "tile"))
    return jax.shard_map(shards, mesh=mesh, in_specs=in_specs, out_specs=out_specs, check_vma=False)
```

time: 73.9 us -> 52.1 us (0.71)
  local copies, waits for them, and re-layouts: 10.9 us -> 0.03 us
  other arithmetic: 9.87 us -> 0 us
  waiting for transfers between devices: 15.4 us -> 7.48 us
  Pallas kernels: 0 us -> 7.77 us
    pallas_call x0 -> x5, Pallas kernels: none -> 7.77 us  [the longest x1 2.56 us: shards(): call(local_substeps, [(flat, F32)] * 2, [(flat, F32)] * 4, flops=20000000)]
    unnamed x21 -> x14, local copies, waits for them, and re-layouts: 6.48 us -> 0.03 us
    all_to_all x3 -> x2, waiting for transfers between devices: 11.1 us -> 5.76 us  [the longest x1 5.75 us: shards(): heats = lax.all_to_all(heats, 'lev', 0, 0, tiled=True)]
    sub x12 -> x0, other arithmetic: 4.55 us -> none  [the longest x6 2.66 us: advance(): pressure[:, :, 1:-1] - courant * (velocity[:, :, 1:] - velocity[:, :, :-1])]
    ppermute x2, waiting for transfers between devices: 4.33 us -> 1.72 us  [the longest x1 1.72 us: shards(): lax.ppermute(to_left, 'tile', [((i + 1) % tiles, i) for i in range(tiles)])]
    all_to_all x3 -> x2, starting transfers between devices: 26 us -> 23.6 us  [the longest x1 16.4 us: shards(): columns = lax.all_to_all(columns, 'lev', 0, 0, tiled=True)]
    ppermute x2, starting transfers between devices: 9.76 us -> 12.2 us  [the longest x1 10.2 us: shards(): lax.ppermute(to_left, 'tile', [((i + 1) % tiles, i) for i in range(tiles)])]
    reshape x1 -> x0, local copies, waits for them, and re-layouts: 1.78 us -> none  [shards(): whole_columns.reshape((whole_columns.shape[0], row_count * portion))]
  transfers between devices with their start and end apart: 5 -> 4, of which waited for: 3 -> 2; matrix products, arithmetic and copies ran while one was open for 17% -> 0% of each run, Pallas kernels for 0% -> 6%
where the time goes in v1:
time: 52.1 us; the launch traced here: 51.8 us
  starting transfers between devices  35.7 us (69%)
  Pallas kernels  7.77 us (15%)
  waiting for transfers between devices  7.48 us (14%)
  between operations  0.74 us (1%)
    all_to_all x1, starting transfers between devices, shards(): columns = lax.all_to_all(columns, 'lev', 0, 0, tiled=True)  16.4 us
    ppermute x1, starting transfers between devices, shards(): lax.ppermute(to_left, 'tile', [((i + 1) % tiles, i) for i in range(tiles)])  10.2 us
    all_to_all x1, starting transfers between devices, shards(): heats = lax.all_to_all(heats, 'lev', 0, 0, tiled=True)  7.21 us
    all_to_all x1, waiting for transfers between devices, shards(): heats = lax.all_to_all(heats, 'lev', 0, 0, tiled=True)  5.75 us
    pallas_call x1, Pallas kernels, shards(): call(local_substeps, [(flat, F32)] * 2, [(flat, F32)] * 4, flops=20000000)  2.56 us
    pallas_call x1, Pallas kernels, shards(): call(finish, [(flat, F32), (flat, F32), (flat, BF16)], [(flat, F32)])  1.95 us
    pallas_call x1, Pallas kernels, shards(): call(send_columns, [((PEERS, FIRST, LANES), BF16)], room=60 << 20)  1.94 us
    ppermute x1, starting transfers between devices, shards(): lax.ppermute(to_right, 'tile', [(i, (i + 1) % tiles) for i in range(tiles)])  1.92 us
  transfers between devices with their start and end apart: 4, of which 2 were waited for; matrix products, arithmetic and copies ran while one was open for 0% of the time, Pallas kernels for 6%

profile of v1, /device:TPU:16, one launch (start us, length us, event | category | flops | bytes accessed | tf_op | source)
XLA Modules:
  0.0 51.8 jit_solution(12828622337436242232)
XLA Ops:
  0.6 0.0 copy-start.1
  0.6 0.0 copy-start.2
  0.7 1.9 %shard_map.94 = bf16[8,80,128]{2,1,0:T(8,128)(2,1)} custom-call(f32[512,128]{1,0:T(8,128)} %bitcast.6, f32[512,128]{1,0:T(8,128)} %bitcast.9), custom_call_target="tpu_custom_call" | custom-call | flops 100000 | bytes 1000000 | tf_op jit(solution)/shard_map/pallas_call | solution.py:238
  2.6 0.0 copy-start
  2.6 0.0 copy-start.4
  2.6 16.4 %all-to-all-start = ((bf16[8,80,128]{2,1,0:T(8,128)(2,1)}), bf16[8,80,128]{2,1,0:T(8,128)(2,1)S(1)}, u32[]{:S(2)}, u32[]{:S(2)}) async-start(bf16[8,80,128]{2,1,0:T(8,128)(2,1)} %shard_map.94), calls=%async_computation | async-start | bytes 327680 | tf_op jit(solution)/shard_map/all_to_all | solution.py:239
  19.0 0.0 copy-done.1
  19.0 0.0 copy-done.2
  19.0 0.0 copy-done
  19.0 0.0 copy-done.4
  19.0 0.0 copy-start.3
  19.0 0.0 copy-start.5
  19.0 0.0 copy-start.6
  19.0 0.3 shard_map.95
  19.4 1.9 %collective-permute-start = (f32[96,128]{1,0:T(8,128)S(1)}, f32[96,128]{1,0:T(8,128)S(1)}, u32[]{:S(2)}, u32[]{:S(2)}) collective-permute-start(f32[96,128]{1,0:T(8,128)S(1)} %get-tuple-element.10), channel_id=1, source_target_pairs={{0,8},{8,16},{16,24},{24,32},{32,40},{40,48},{48,56},{56,64},{64,7... | collective-permute-start | bytes 147464 | tf_op jit(solution)/shard_map/ppermute | solution.py:243
  21.3 10.2 %collective-permute-start.1 = (f32[96,128]{1,0:T(8,128)S(1)}, f32[96,128]{1,0:T(8,128)S(1)}, u32[]{:S(2)}, u32[]{:S(2)}) collective-permute-start(f32[96,128]{1,0:T(8,128)S(1)} %get-tuple-element.11), channel_id=1, source_target_pairs={{8,0},{16,8},{24,16},{32,24},{40,32},{48,40},{56,48},{64,56},{72,6... | collective-permute-start | bytes 147464 | tf_op jit(solution)/shard_map/ppermute | solution.py:244
  31.6 0.0 collective-permute-done.from_left
  31.6 1.7 %collective-permute-done.1.from_right = f32[96,128]{1,0:T(8,128)S(1)} collective-permute-done((f32[96,128]{1,0:T(8,128)S(1)}, f32[96,128]{1,0:T(8,128)S(1)}, u32[]{:S(2)}, u32[]{:S(2)}) %collective-permute-start.1) | collective-permute-done | bytes 49184 | tf_op jit(solution)/shard_map/ppermute | solution.py:244
  33.3 0.0 all-to-all-done.got
  33.3 0.0 copy-done.3
  33.3 0.0 copy-done.5
  33.3 0.0 copy-done.6
  33.3 1.0 %shard_map.96 = bf16[8,96,128]{2,1,0:T(8,128)(2,1)} custom-call(bf16[8,80,128]{2,1,0:T(8,128)(2,1)S(1)} %all-to-all-done.got, s32[32,128]{1,0:T(8,128)S(1)} %copy-done.5, s32[32,128]{1,0:T(8,128)S(1)} %copy-done.6, bf16[4,128,128]{2,1,0:T(8,128)(2,1)S(1)} %copy-done.3, f32[96,128]{1,0:T(8,128)S(1)} %collective-permute-done.from_left, ...), custom_call_target="tpu_custom_call" | custom-call | flops 70000000 | bytes 1000000 | tf_op jit(solution)/shard_map/pallas_call | solution.py:245
  34.3 7.2 %all-to-all-start.1 = ((bf16[8,96,128]{2,1,0:T(8,128)(2,1)}), bf16[8,96,128]{2,1,0:T(8,128)(2,1)S(1)}, u32[]{:S(2)}, u32[]{:S(2)}) async-start(bf16[8,96,128]{2,1,0:T(8,128)(2,1)} %shard_map.96), calls=%async_computation.1 | async-start | bytes 393216 | tf_op jit(solution)/shard_map/all_to_all | solution.py:248
  41.5 2.6 %shard_map.97 = (f32[512,128]{1,0:T(8,128)S(1)}, f32[512,128]{1,0:T(8,128)S(1)}) custom-call(f32[512,128]{1,0:T(8,128)S(1)} %bitcast.8, f32[512,128]{1,0:T(8,128)S(1)} %bitcast.11, f32[512,128]{1,0:T(8,128)S(1)} %bitcast.13, f32[32,128]{1,0:T(8,128)S(1)} %copy-done.4, f32[96,128]{1,0:T(8,128)S(1)} %collective-permute-done.from_left, ...), custom_call_target="tpu_custom_call" | custom-call | flops 20000000 | bytes 1000000 | tf_op jit(solution)/shard_map/pallas_call | solution.py:249
  44.1 5.8 %all-to-all-done.1.got = bf16[8,96,128]{2,1,0:T(8,128)(2,1)S(1)} async-done(((bf16[8,96,128]{2,1,0:T(8,128)(2,1)}), bf16[8,96,128]{2,1,0:T(8,128)(2,1)S(1)}, u32[]{:S(2)}, u32[]{:S(2)}) %all-to-all-start.1) | async-done | bytes 196640 | tf_op jit(solution)/shard_map/all_to_all | solution.py:248
  49.8 1.9 %shard_map.98 = (f32[512,128]{1,0:T(8,128)}, f32[512,128]{1,0:T(8,128)}, bf16[512,128]{1,0:T(8,128)(2,1)}) custom-call(bf16[8,96,128]{2,1,0:T(8,128)(2,1)S(1)} %all-to-all-done.1.got, f32[512,128]{1,0:T(8,128)S(1)} %get-tuple-element.12.local_p, f32[512,128]{1,0:T(8,128)S(1)} %get-tuple-element.13.local_w), custom_call_target="tpu_custom_call" | custom-call | flops 100000 | bytes 1000000 | tf_op jit(solution)/shard_map/pallas_call | solution.py:252
Async XLA Ops:
  0.6 18.3 %copy-start.1 = (f32[16,32,128]{2,1,0:T(8,128)S(1)}, f32[16,32,128]{2,1,0:T(8,128)}, u32[]{:S(2)}) copy-start(f32[16,32,128]{2,1,0:T(8,128)} %param.8) | copy-start | bytes 786436
  0.6 18.3 %copy-start.2 = (f32[16,32,128]{2,1,0:T(8,128)S(1)}, f32[16,32,128]{2,1,0:T(8,128)}, u32[]{:S(2)}) copy-start(f32[16,32,128]{2,1,0:T(8,128)} %param.9) | copy-start | bytes 786436
  2.6 16.4 %copy-start = (f32[16,32,128]{2,1,0:T(8,128)S(1)}, f32[16,32,128]{2,1,0:T(8,128)}, u32[]{:S(2)}) copy-start(f32[16,32,128]{2,1,0:T(8,128)} %param.7) | copy-start | bytes 786436
  2.6 16.4 %copy-start.4 = (f32[32,128]{1,0:T(8,128)S(1)}, f32[32,128]{1,0:T(8,128)}, u32[]{:S(2)}) copy-start(f32[32,128]{1,0:T(8,128)} %surface.3) | copy-start | bytes 49156
  2.6 30.7 %all-to-all-start = ((bf16[8,80,128]{2,1,0:T(8,128)(2,1)}), bf16[8,80,128]{2,1,0:T(8,128)(2,1)S(1)}, u32[]{:S(2)}, u32[]{:S(2)}) async-start(bf16[8,80,128]{2,1,0:T(8,128)(2,1)} %shard_map.94), calls=%async_computation | async-start | bytes 327680 | tf_op jit(solution)/shard_map/all_to_all | solution.py:239
  19.0 14.3 %copy-start.3 = (bf16[4,128,128]{2,1,0:T(8,128)(2,1)S(1)}, bf16[4,128,128]{2,1,0:T(8,128)(2,1)}, u32[]{:S(2)}) copy-start(bf16[4,128,128]{2,1,0:T(8,128)(2,1)} %weights.1) | copy-start | bytes 393220
  19.0 14.3 %copy-start.5 = (s32[32,128]{1,0:T(8,128)S(1)}, s32[32,128]{1,0:T(8,128)}, u32[]{:S(2)}) copy-start(s32[32,128]{1,0:T(8,128)} %trigger.1) | copy-start | bytes 49156
  19.0 14.3 %copy-start.6 = (s32[32,128]{1,0:T(8,128)S(1)}, s32[32,128]{1,0:T(8,128)}, u32[]{:S(2)}) copy-start(s32[32,128]{1,0:T(8,128)} %closure.1) | copy-start | bytes 49156
  19.4 12.2 %collective-permute-start = (f32[96,128]{1,0:T(8,128)S(1)}, f32[96,128]{1,0:T(8,128)S(1)}, u32[]{:S(2)}, u32[]{:S(2)}) collective-permute-start(f32[96,128]{1,0:T(8,128)S(1)} %get-tuple-element.10), channel_id=1, source_target_pairs={{0,8},{8,16},{16,24},{24,32},{32,40},{40,48},{48,56},{56,64},{64,7... | collective-permute-start | bytes 147464 | tf_op jit(solution)/shard_map/ppermute | solution.py:243
  21.3 12.0 %collective-permute-start.1 = (f32[96,128]{1,0:T(8,128)S(1)}, f32[96,128]{1,0:T(8,128)S(1)}, u32[]{:S(2)}, u32[]{:S(2)}) collective-permute-start(f32[96,128]{1,0:T(8,128)S(1)} %get-tuple-element.11), channel_id=1, source_target_pairs={{8,0},{16,8},{24,16},{32,24},{40,32},{48,40},{56,48},{64,56},{72,6... | collective-permute-start | bytes 147464 | tf_op jit(solution)/shard_map/ppermute | solution.py:244
  34.3 15.5 %all-to-all-start.1 = ((bf16[8,96,128]{2,1,0:T(8,128)(2,1)}), bf16[8,96,128]{2,1,0:T(8,128)(2,1)S(1)}, u32[]{:S(2)}, u32[]{:S(2)}) async-start(bf16[8,96,128]{2,1,0:T(8,128)(2,1)} %shard_map.96), calls=%async_computation.1 | async-start | bytes 393216 | tf_op jit(solution)/shard_map/all_to_all | solution.py:248

commit v2 on v1

v2 whole, which is shorter than its diff:
```python
import jax
import jax.numpy as jnp
from jax import lax
from jax.experimental import pallas as pl
from jax.experimental.pallas import tpu as pltpu
from jax.sharding import PartitionSpec as P


LEVELS = 128
SUBSTEPS = 6
COURANT = 0.9
SCALE = LEVELS ** (-0.5)
PEERS = 8
OWN = 16
ROWS = 32
LANES = 128
BAND = 4
PIECE = 88
BF16 = jnp.bfloat16
F32 = jnp.float32


def lanes_of(shape):
    return lax.broadcasted_iota(jnp.int32, shape, len(shape) - 1)


def rows_of(shape):
    return lax.broadcasted_iota(jnp.int32, shape, len(shape) - 2)


def turned(x, shift):
    return pltpu.roll(x, shift % LANES, 1)


def three_parts(x):
    high = x.astype(BF16).astype(F32)
    rest = x - high
    middle = rest.astype(BF16).astype(F32)
    return high, middle, rest - middle


def sub(a, b):
    return a - COURANT * b


def substeps(pressure, wind):
    for _ in range(SUBSTEPS):
        wind = sub(wind, turned(pressure, -1) - pressure)
        pressure = sub(pressure, wind - turned(wind, 1))
    return pressure, wind


def windowed(main, left, right):
    lane = lanes_of(main.shape)
    return jnp.where(
        lane < 6,
        left,
        jnp.where(lane < 32, turned(main, 6), jnp.where(lane < 76, turned(main, 76), right)),
    )


def edges_in(main, window):
    lane = lanes_of(main.shape)
    return jnp.where(
        lane < 6, turned(window, -6), jnp.where(lane >= 122, turned(window, 52), main)
    )


def odd_tile():
    return lax.rem(lax.axis_index("tile"), 2) == 1


def by_side(right, if_right, if_left):
    return jnp.where(right, if_right % LANES, if_left % LANES)


def swung(x, right, if_right, if_left):
    return pltpu.roll(x, by_side(right, if_right, if_left), 1)


def folded(border):
    kept = jnp.where(lanes_of(border.shape) < 6, border, 0.0)
    out = kept[0:8]
    for group in range(1, 4):
        out = out + turned(kept[8 * group : 8 * group + 8], 8 * group)
    return out


def unfolded(fold):
    return jnp.concatenate([turned(fold, -8 * group) for group in range(4)])


def halves_swapped(x):
    return pltpu.roll(x, 4, 0)


def in_low_half(fold):
    return halves_swapped(fold) + turned(fold, 32)


def from_low_half(fold):
    top = rows_of(fold.shape) < 4
    return jnp.where(top, halves_swapped(fold), turned(fold, -32))


def top_half():
    return rows_of((8, LANES)) < 4


def send_parts(out, peer, x):
    high, middle, low = three_parts(x)
    out[peer, 64:80, :] = jnp.concatenate([high, middle]).astype(BF16)
    out[peer, 80:88, :] = low.astype(BF16)


def got_parts(got, peer):
    pair = got[peer, 64:80, :].astype(F32)
    return (pair[0:8] + pair[8:16]) + got[peer, 80:88, :].astype(F32)


def send_columns(theta, thickness, out):
    total = jnp.zeros((ROWS, LANES), F32)
    for level in range(OWN):
        at = pl.ds(level * ROWS, ROWS)
        total = total + theta[at, :] * thickness[at, :] * SCALE
    for row in range(ROWS):
        picked = theta[pl.ds(row, OWN, stride=ROWS), :]
        out[row // BAND, pl.ds(OWN * (row % BAND), OWN), :] = picked.astype(BF16)
    border = in_low_half(folded(swung(total, odd_tile(), -122, 0)))
    for group in range(4):
        rows = total[8 * group : 8 * group + 8]
        send_parts(out, 2 * group, jnp.where(top_half(), rows, border))
        send_parts(out, 2 * group + 1, jnp.where(top_half(), halves_swapped(rows), border))


def send_borders(theta, thickness, wind, surface, to_chip, to_core):
    lane = lanes_of((ROWS, LANES))
    zero = jnp.zeros((ROWS, LANES), F32)
    ground = surface[...]
    below = zero
    packed = [[zero, zero], [zero, zero]]
    for level in reversed(range(OWN)):
        at = pl.ds(level * ROWS, ROWS)
        thermal = theta[at, :] * thickness[at, :] * SCALE
        fields = (ground + (below + 0.5 * thermal), wind[at, :])
        below = below + thermal
        here = (lane >= 8 * level) & (lane < 8 * level + 8)
        for index, field in enumerate(fields):
            packed[0][index] = jnp.where(here, turned(field, 8 * level - 122), packed[0][index])
            packed[1][index] = jnp.where(here, turned(field, 8 * level), packed[1][index])
    odd = odd_tile()
    for index in range(2):
        at = pl.ds(ROWS * index, ROWS)
        to_chip[at, :] = jnp.where(odd, packed[0][index], packed[1][index])
        to_core[at, :] = jnp.where(odd, packed[1][index], packed[0][index])
    to_core[64:72, :] = folded(swung(below, odd, 0, -122))


def send_heating(got, trigger, closure, weights, from_core, raw, out, to_chip, stacked):
    me = lax.axis_index("lev")
    flags = trigger[pl.ds(BAND * me, BAND), :].astype(F32)
    scheme = closure[pl.ds(BAND * me, BAND), :]
    for row in range(BAND):
        chosen = [
            jnp.broadcast_to(
                jnp.where(scheme[row : row + 1] == s, flags[row : row + 1], 0.0), (OWN, LANES)
            ).astype(BF16)
            for s in range(3)
        ]
        columns = pl.ds(LANES * row, LANES)
        for peer in range(PEERS):
            block = got[peer, pl.ds(OWN * row, OWN), :]
            for s in range(3):
                stacked[pl.ds(LEVELS * s + OWN * peer, OWN), columns] = block * chosen[s]
            stacked[pl.ds(LEVELS * 3 + OWN * peer, OWN), columns] = block
    wide = jnp.concatenate([weights[s] for s in range(4)], axis=1)
    answer = jnp.dot(wide, stacked[...], preferred_element_type=F32).astype(BF16)
    for peer in range(PEERS):
        for row in range(BAND):
            out[peer, pl.ds(OWN * row, OWN), :] = answer[
                OWN * peer : OWN * peer + OWN, LANES * row : LANES * row + LANES
            ]
    core_border = in_low_half(from_core[64:72, :])
    higher = jnp.zeros((8, LANES), F32)
    beyond = jnp.zeros((8, LANES), F32)
    for peer in reversed(range(PEERS)):
        send_parts(out, peer, jnp.where(top_half(), higher, core_border))
        part = got_parts(got, peer)
        higher = higher + part
        beyond = beyond + jnp.where(me < peer, 1.0, 0.0) * part
    to_chip[0:64, :] = raw[...]
    to_chip[64:72, :] = from_low_half(beyond)


def slot(level):
    return 32 * (level % 4)


def local_substeps(
    theta, thickness, wind, surface, from_core, out_p, out_w, chip_p, chip_w, core_p, core_w
):
    chip_right = odd_tile()
    core_right = jnp.logical_not(chip_right)
    lane = lanes_of((ROWS, LANES))
    ground = surface[...]
    below = jnp.zeros((ROWS, LANES), F32)
    halo_from = by_side(core_right, 12, 0)
    is_halo = ((lane & 31) >= halo_from) & ((lane & 31) < halo_from + 6)
    halos = [from_core[0:32, :], from_core[32:64, :]]
    packed = None
    for level in reversed(range(OWN)):
        at = pl.ds(level * ROWS, ROWS)
        thermal = theta[at, :] * thickness[at, :] * SCALE
        fields = (ground + (below + 0.5 * thermal), wind[at, :])
        below = below + thermal
        out_p[at, :] = fields[0]
        here = slot(level)
        if level % 4 == 3:
            packed = [jnp.zeros((ROWS, LANES), F32)] * 4
        mine = (lane >= here) & (lane < here + 32)
        for i in range(2):
            for j, right in ((0, chip_right), (2, core_right)):
                side = swung(fields[i], right, here - 116, here + 6)
                if j == 2:
                    halo = swung(halos[i], right, here + 12 - 8 * level, here - 8 * level)
                    side = jnp.where(is_halo, halo, side)
                packed[i + j] = jnp.where(mine, side, packed[i + j])
        if level % 4 == 0:
            group = pl.ds(8 * level, ROWS)
            for ref, value in zip((chip_p, chip_w, core_p, core_w), packed):
                ref[group, :] = value
    p, w = substeps(out_p[...], wind[...])
    out_p[...] = p
    out_w[...] = w
    p, w = substeps(core_p[...], core_w[...])
    core_p[...] = p
    core_w[...] = w
    fix_edges(out_p, out_w, core_p, core_w, core_right, out_p, out_w, 0.0, 0.0)


def fix_edges(base_p, base_w, edge_p, edge_w, right, out_p, out_w, add_p, add_w):
    lane = lanes_of((ROWS, LANES))
    start = by_side(right, 122, 0)
    fixed = (lane >= start) & (lane < start + 6)
    for level in range(OWN):
        at = pl.ds(level * ROWS, ROWS)
        group = pl.ds(ROWS * (level // 4), ROWS)
        here = slot(level)
        for base, edge, out, add in (
            (base_p, edge_p, out_p, add_p),
            (base_w, edge_w, out_w, add_w),
        ):
            moved = swung(edge[group, :], right, 116 - here, -6 - here)
            out[at, :] = jnp.where(fixed, moved, base[at, :]) + add


def spread_heating(got, out_h, out_sum, rows_first):
    me = lax.axis_index("lev")
    beyond = jnp.zeros((8, LANES), F32)
    pieces = []
    for peer in range(PEERS):
        piece = got_parts(got, peer)
        pieces.append(piece)
        beyond = beyond + jnp.where(me < peer, 1.0, 0.0) * piece
    for group in range(4):
        out_sum[8 * group : 8 * group + 8, :] = jnp.where(
            top_half(), pieces[2 * group], halves_swapped(pieces[2 * group + 1])
        )
    out_sum[32:64, :] = unfolded(from_low_half(beyond))
    for peer in range(PEERS):
        rows_first[pl.ds(64 * peer, 64), :] = got[peer, 0:64, :].astype(F32)
    for level in range(OWN):
        out_h[pl.ds(level * ROWS, ROWS), :] = rows_first[pl.ds(level, ROWS, stride=OWN), :].astype(
            BF16
        )


def finish(from_chip, sums, local_p, local_w, chip_p, chip_w, out_p, out_w, edge_p, edge_w):
    right = odd_tile()
    lane = lanes_of((ROWS, LANES))
    halo_from = by_side(right, 12, 0)
    is_halo = ((lane & 31) >= halo_from) & ((lane & 31) < halo_from + 6)
    for base, edge, first in ((chip_p, edge_p, 0), (chip_w, edge_w, 32)):
        halos = from_chip[first : first + 32, :]
        for group in range(4):
            at = pl.ds(ROWS * group, ROWS)
            value = base[at, :]
            for level in range(4 * group, 4 * group + 4):
                here = slot(level)
                mine = is_halo & (lane >= here) & (lane < here + 32)
                halo = swung(halos, right, here + 12 - 8 * level, here - 8 * level)
                value = jnp.where(mine, halo, value)
            edge[at, :] = value
    p, w = substeps(edge_p[...], edge_w[...])
    edge_p[...] = p
    edge_w[...] = w
    main = sums[0:32, :]
    core = sums[32:64, :]
    chip = unfolded(from_chip[64:72, :])
    side = windowed(
        main, jnp.where(right, core, chip), turned(jnp.where(right, chip, core), 76)
    )
    zero = jnp.zeros((ROWS, LANES), F32)
    add_p, add_w = substeps(main, zero)
    side_p, side_w = substeps(side, zero)
    fix_edges(
        local_p, local_w, edge_p, edge_w, right, out_p, out_w, edges_in(add_p, side_p), edges_in(add_w, side_w)
    )


def call(kernel, outs, scratch=(), flops=100000, moved=1000000, room=8 << 20):
    return pl.pallas_call(
        kernel,
        out_shape=tuple(jax.ShapeDtypeStruct(s, d) for s, d in outs),
        scratch_shapes=[pltpu.VMEM(s, d) for s, d in scratch],
        compiler_params=pltpu.CompilerParams(vmem_limit_bytes=room),
        cost_estimate=pl.CostEstimate(flops=flops, bytes_accessed=moved, transcendentals=0),
    )


def coupled(theta, thickness, wind, surface, trigger, closure, closure_weights):
    flat = (OWN * ROWS, LANES)
    theta, thickness, wind = (x.reshape(flat) for x in (theta, thickness, wind))
    tiles = lax.axis_size("tile")
    (columns,) = call(send_columns, [((PEERS, PIECE, LANES), BF16)], room=60 << 20)(
        theta, thickness
    )
    columns = lax.all_to_all(columns, "lev", 0, 0, tiled=True)
    raw, to_core = call(send_borders, [((64, LANES), F32), ((72, LANES), F32)])(
        theta, thickness, wind, surface
    )
    between = [((t + 1) % tiles, (t + 2) % tiles) for t in range(0, tiles, 2)]
    within = [(t, t + 1) for t in range(0, tiles, 2)]
    from_core = lax.ppermute(to_core, "tile", within + [(b, a) for a, b in within])
    heats, to_chip = call(
        send_heating,
        [((PEERS, PIECE, LANES), BF16), ((72, LANES), F32)],
        [((512, 512), BF16)],
        flops=70000000,
    )(columns, trigger, closure, closure_weights, from_core, raw)
    heats = lax.all_to_all(heats, "lev", 0, 0, tiled=True)
    from_chip = lax.ppermute(to_chip, "tile", between + [(b, a) for a, b in between])
    packed = (4 * ROWS, LANES)
    local_p, local_w, chip_p, chip_w = call(
        local_substeps,
        [(flat, F32)] * 2 + [(packed, F32)] * 2,
        [(packed, F32)] * 2,
        flops=20000000,
    )(theta, thickness, wind, surface, from_core)
    heating, sums = call(
        spread_heating, [(flat, BF16), ((64, LANES), F32)], [(flat, F32)]
    )(heats)
    pressure, wind_next = call(finish, [(flat, F32)] * 2, [(packed, F32)] * 2)(
        from_chip, sums, local_p, local_w, chip_p, chip_w
    )
    shape = (OWN, ROWS, LANES)
    return pressure.reshape(shape), wind_next.reshape(shape), heating.reshape(shape)


def solution(mesh):
    in_specs = (
        P("lev", None, "tile"),
        P("lev", None, "tile"),
        P("lev", None, "tile"),
        P(None, "tile"),
        P(None, "tile"),
        P(None, "tile"),
        P(),
    )
    out_specs = (P("lev", None, "tile"), P("lev", None, "tile"), P("lev", None, "tile"))
    return jax.shard_map(
        coupled, mesh=mesh, in_specs=in_specs, out_specs=out_specs, check_vma=False
    )
```

time: 52.1 us -> 47.9 us (0.919)
  starting transfers between devices: 35.7 us -> 32.4 us
  waiting for transfers between devices: 7.48 us -> 5.81 us
  Pallas kernels: 7.77 us -> 8.56 us
    all_to_all x2, starting transfers between devices: 23.6 us -> 21.1 us  [the longest x1 16.4 us: coupled(): columns = lax.all_to_all(columns, 'lev', 0, 0, tiled=True)]
    all_to_all x2, waiting for transfers between devices: 5.76 us -> 4.63 us  [the longest x1 4.62 us: coupled(): columns = lax.all_to_all(columns, 'lev', 0, 0, tiled=True)]
    ppermute x2, starting transfers between devices: 12.2 us -> 11.3 us  [the longest x1 9.33 us: coupled(): lax.ppermute(to_chip, 'tile', between + [(b, a) for a, b in between])]
    pallas_call x5 -> x6, Pallas kernels: 7.77 us -> 8.56 us  [the longest x1 2.19 us: coupled(): call(finish, [(flat, F32)] * 2, [(packed, F32)] * 2)]
    ppermute x2, waiting for transfers between devices: 1.72 us -> 1.18 us  [the longest x1 1.18 us: coupled(): lax.ppermute(to_core, 'tile', within + [(b, a) for a, b in within])]
  transfers between devices with their start and end apart: 4 -> 4, of which waited for: 2 -> 2; matrix products, arithmetic and copies ran while one was open for 0% -> 0% of each run, Pallas kernels for 6% -> 7%
where the time goes in v2:
time: 47.9 us; the launch traced here: 47.5 us
  starting transfers between devices  32.4 us (68%)
  Pallas kernels  8.56 us (18%)
  waiting for transfers between devices  5.81 us (12%)
  between operations  0.74 us (2%)
    all_to_all x1, starting transfers between devices, coupled(): columns = lax.all_to_all(columns, 'lev', 0, 0, tiled=True)  16.4 us
    ppermute x1, starting transfers between devices, coupled(): lax.ppermute(to_chip, 'tile', between + [(b, a) for a, b in between])  9.33 us
    all_to_all x1, starting transfers between devices, coupled(): heats = lax.all_to_all(heats, 'lev', 0, 0, tiled=True)  4.74 us
    all_to_all x1, waiting for transfers between devices, coupled(): columns = lax.all_to_all(columns, 'lev', 0, 0, tiled=True)  4.62 us
    pallas_call x1, Pallas kernels, coupled(): call(finish, [(flat, F32)] * 2, [(packed, F32)] * 2)  2.19 us
    pallas_call x1, Pallas kernels, coupled(): call(local_substeps, [(flat, F32)] * 2 + [(packed, F32)] * 2, [(packed, F...  2.16 us
    pallas_call x1, Pallas kernels, coupled(): call(send_columns, [((PEERS, PIECE, LANES), BF16)], room=60 << 20)  2.07 us
    ppermute x1, starting transfers between devices, coupled(): lax.ppermute(to_core, 'tile', within + [(b, a) for a, b in within])  1.92 us
  transfers between devices with their start and end apart: 4, of which 2 were waited for; matrix products, arithmetic and copies ran while one was open for 0% of the time, Pallas kernels for 7%

profile of v2, /device:TPU:16, one launch (start us, length us, event | category | flops | bytes accessed | tf_op | source)
XLA Modules:
  0.0 47.5 jit_solution(9781781333226181740)
XLA Ops:
  0.6 0.0 copy-start.1
  0.6 0.0 copy-start.2
  0.7 2.1 %shard_map.94 = bf16[8,88,128]{2,1,0:T(8,128)(2,1)} custom-call(f32[512,128]{1,0:T(8,128)} %bitcast.6, f32[512,128]{1,0:T(8,128)} %bitcast.9), custom_call_target="tpu_custom_call" | custom-call | flops 100000 | bytes 1000000 | tf_op jit(solution)/shard_map/pallas_call | solution.py:325
  2.7 0.0 copy-start
  2.7 0.0 copy-start.4
  2.7 16.4 %all-to-all-start = ((bf16[8,88,128]{2,1,0:T(8,128)(2,1)}), bf16[8,88,128]{2,1,0:T(8,128)(2,1)S(1)}, u32[]{:S(2)}, u32[]{:S(2)}) async-start(bf16[8,88,128]{2,1,0:T(8,128)(2,1)} %shard_map.94), calls=%async_computation | async-start | bytes 360448 | tf_op jit(solution)/shard_map/all_to_all | solution.py:328
  19.1 0.0 copy-done.1
  19.1 0.0 copy-done.2
  19.1 0.0 copy-done
  19.1 0.0 copy-done.4
  19.1 0.0 copy-start.3
  19.1 0.0 copy-start.5
  19.2 0.0 copy-start.6
  19.2 0.4 shard_map.95
  19.5 1.9 %collective-permute-start = (f32[72,128]{1,0:T(8,128)S(1)}, f32[72,128]{1,0:T(8,128)S(1)}, u32[]{:S(2)}, u32[]{:S(2)}) collective-permute-start(f32[72,128]{1,0:T(8,128)S(1)} %get-tuple-element.15), channel_id=1, source_target_pairs={{0,8},{16,24},{32,40},{48,56},{64,72},{80,88},{96,104},{112,120},{... | collective-permute-start | bytes 110600 | tf_op jit(solution)/shard_map/ppermute | solution.py:334
  21.5 1.2 %collective-permute-done.from_core = f32[72,128]{1,0:T(8,128)S(1)} collective-permute-done((f32[72,128]{1,0:T(8,128)S(1)}, f32[72,128]{1,0:T(8,128)S(1)}, u32[]{:S(2)}, u32[]{:S(2)}) %collective-permute-start) | collective-permute-done | bytes 36896 | tf_op jit(solution)/shard_map/ppermute | solution.py:334
  22.7 4.6 %all-to-all-done.got = bf16[8,88,128]{2,1,0:T(8,128)(2,1)S(1)} async-done(((bf16[8,88,128]{2,1,0:T(8,128)(2,1)}), bf16[8,88,128]{2,1,0:T(8,128)(2,1)S(1)}, u32[]{:S(2)}, u32[]{:S(2)}) %all-to-all-start) | async-done | bytes 180256 | tf_op jit(solution)/shard_map/all_to_all | solution.py:328
  27.3 0.0 copy-done.3
  27.3 0.0 copy-done.5
  27.3 0.0 copy-done.6
  27.3 1.0 %shard_map.96 = (bf16[8,88,128]{2,1,0:T(8,128)(2,1)}, f32[72,128]{1,0:T(8,128)S(1)}) custom-call(bf16[8,88,128]{2,1,0:T(8,128)(2,1)S(1)} %all-to-all-done.got, s32[32,128]{1,0:T(8,128)S(1)} %copy-done.5, s32[32,128]{1,0:T(8,128)S(1)} %copy-done.6, bf16[4,128,128]{2,1,0:T(8,128)(2,1)S(1)} %copy-done.3, f32[72,128]{1,0:T(8,128)S(1)} %collective-permute-done.from_core, ...), custom_call_target="tpu_custom_call" | custom-call | flops 70000000 | bytes 1000000 | tf_op jit(solution)/shard_map/pallas_call | solution.py:335
  28.3 4.7 %all-to-all-start.1 = ((bf16[8,88,128]{2,1,0:T(8,128)(2,1)}), bf16[8,88,128]{2,1,0:T(8,128)(2,1)S(1)}, u32[]{:S(2)}, u32[]{:S(2)}) async-start(bf16[8,88,128]{2,1,0:T(8,128)(2,1)} %get-tuple-element.18), calls=%async_computation.1 | async-start | bytes 360448 | tf_op jit(solution)/shard_map/all_to_all | solution.py:341
  33.0 9.3 %collective-permute-start.1 = (f32[72,128]{1,0:T(8,128)S(1)}, f32[72,128]{1,0:T(8,128)S(1)}, u32[]{:S(2)}, u32[]{:S(2)}) collective-permute-start(f32[72,128]{1,0:T(8,128)S(1)} %get-tuple-element.17), channel_id=1, source_target_pairs={{8,16},{24,32},{40,48},{56,64},{72,80},{88,96},{104,112},{120,128}... | collective-permute-start | bytes 110600 | tf_op jit(solution)/shard_map/ppermute | solution.py:342
  42.3 2.2 %shard_map.98 = (f32[512,128]{1,0:T(8,128)S(1)}, f32[512,128]{1,0:T(8,128)S(1)}, f32[128,128]{1,0:T(8,128)S(1)}, f32[128,128]{1,0:T(8,128)S(1)}) custom-call(f32[512,128]{1,0:T(8,128)S(1)} %bitcast.8, f32[512,128]{1,0:T(8,128)S(1)} %bitcast.11, f32[512,128]{1,0:T(8,128)S(1)} %bitcast.13, f32[32,128]{1,0:T(8,128)S(1)} %copy-done.4, ...), custom_call_target="tpu_custom_call" | custom-call | flops 20000000 | bytes 1000000 | tf_op jit(solution)/shard_map/pallas_call | solution.py:344
  44.5 0.0 all-to-all-done.1.got
  44.5 0.8 %shard_map.97 = (bf16[512,128]{1,0:T(8,128)(2,1)}, f32[64,128]{1,0:T(8,128)S(1)}) custom-call(bf16[8,88,128]{2,1,0:T(8,128)(2,1)S(1)} %all-to-all-done.1.got), custom_call_target="tpu_custom_call" | custom-call | flops 100000 | bytes 1000000 | tf_op jit(solution)/shard_map/pallas_call | solution.py:350
  45.3 0.0 collective-permute-done.1.from_chip
  45.3 2.2 %shard_map.99 = (f32[512,128]{1,0:T(8,128)}, f32[512,128]{1,0:T(8,128)}) custom-call(f32[72,128]{1,0:T(8,128)S(1)} %collective-permute-done.1.from_chip, f32[64,128]{1,0:T(8,128)S(1)} %get-tuple-element.19.sums, f32[512,128]{1,0:T(8,128)S(1)} %get-tuple-element.20.local_p, f32[512,128]{1,0:T(8,128)S(1)} %get-tuple-element.21.local_w, ...), custom_call_target="tpu_custom_call" | custom-call | flops 100000 | bytes 1000000 | tf_op jit(solution)/shard_map/pallas_call | solution.py:353
Async XLA Ops:
  0.6 18.5 %copy-start.1 = (f32[16,32,128]{2,1,0:T(8,128)S(1)}, f32[16,32,128]{2,1,0:T(8,128)}, u32[]{:S(2)}) copy-start(f32[16,32,128]{2,1,0:T(8,128)} %param.8) | copy-start | bytes 786436
  0.6 18.5 %copy-start.2 = (f32[16,32,128]{2,1,0:T(8,128)S(1)}, f32[16,32,128]{2,1,0:T(8,128)}, u32[]{:S(2)}) copy-start(f32[16,32,128]{2,1,0:T(8,128)} %param.9) | copy-start | bytes 786436
  2.7 16.4 %copy-start = (f32[16,32,128]{2,1,0:T(8,128)S(1)}, f32[16,32,128]{2,1,0:T(8,128)}, u32[]{:S(2)}) copy-start(f32[16,32,128]{2,1,0:T(8,128)} %param.7) | copy-start | bytes 786436
  2.7 16.4 %copy-start.4 = (f32[32,128]{1,0:T(8,128)S(1)}, f32[32,128]{1,0:T(8,128)}, u32[]{:S(2)}) copy-start(f32[32,128]{1,0:T(8,128)} %surface.3) | copy-start | bytes 49156
  2.7 24.6 %all-to-all-start = ((bf16[8,88,128]{2,1,0:T(8,128)(2,1)}), bf16[8,88,128]{2,1,0:T(8,128)(2,1)S(1)}, u32[]{:S(2)}, u32[]{:S(2)}) async-start(bf16[8,88,128]{2,1,0:T(8,128)(2,1)} %shard_map.94), calls=%async_computation | async-start | bytes 360448 | tf_op jit(solution)/shard_map/all_to_all | solution.py:328
  19.1 8.1 %copy-start.3 = (bf16[4,128,128]{2,1,0:T(8,128)(2,1)S(1)}, bf16[4,128,128]{2,1,0:T(8,128)(2,1)}, u32[]{:S(2)}) copy-start(bf16[4,128,128]{2,1,0:T(8,128)(2,1)} %weights.1) | copy-start | bytes 393220
  19.1 8.1 %copy-start.5 = (s32[32,128]{1,0:T(8,128)S(1)}, s32[32,128]{1,0:T(8,128)}, u32[]{:S(2)}) copy-start(s32[32,128]{1,0:T(8,128)} %trigger.1) | copy-start | bytes 49156
  19.2 8.1 %copy-start.6 = (s32[32,128]{1,0:T(8,128)S(1)}, s32[32,128]{1,0:T(8,128)}, u32[]{:S(2)}) copy-start(s32[32,128]{1,0:T(8,128)} %closure.1) | copy-start | bytes 49156
  19.5 3.1 %collective-permute-start = (f32[72,128]{1,0:T(8,128)S(1)}, f32[72,128]{1,0:T(8,128)S(1)}, u32[]{:S(2)}, u32[]{:S(2)}) collective-permute-start(f32[72,128]{1,0:T(8,128)S(1)} %get-tuple-element.15), channel_id=1, source_target_pairs={{0,8},{16,24},{32,40},{48,56},{64,72},{80,88},{96,104},{112,120},{... | collective-permute-start | bytes 110600 | tf_op jit(solution)/shard_map/ppermute | solution.py:334
  28.3 16.3 %all-to-all-start.1 = ((bf16[8,88,128]{2,1,0:T(8,128)(2,1)}), bf16[8,88,128]{2,1,0:T(8,128)(2,1)S(1)}, u32[]{:S(2)}, u32[]{:S(2)}) async-start(bf16[8,88,128]{2,1,0:T(8,128)(2,1)} %get-tuple-element.18), calls=%async_computation.1 | async-start | bytes 360448 | tf_op jit(solution)/shard_map/all_to_all | solution.py:341
  33.0 12.3 %collective-permute-start.1 = (f32[72,128]{1,0:T(8,128)S(1)}, f32[72,128]{1,0:T(8,128)S(1)}, u32[]{:S(2)}, u32[]{:S(2)}) collective-permute-start(f32[72,128]{1,0:T(8,128)S(1)} %get-tuple-element.17), channel_id=1, source_target_pairs={{8,16},{24,32},{40,48},{56,64},{72,80},{88,96},{104,112},{120,128}... | collective-permute-start | bytes 110600 | tf_op jit(solution)/shard_map/ppermute | solution.py:342

commit v3 on v2

--- a/solution.py
+++ b/solution.py
@@ -50,20 +50,14 @@
     return pressure, wind
 
 
-def windowed(main, left, right):
-    lane = lanes_of(main.shape)
-    return jnp.where(
-        lane < 6,
-        left,
-        jnp.where(lane < 32, turned(main, 6), jnp.where(lane < 76, turned(main, 76), right)),
-    )
-
-
-def edges_in(main, window):
-    lane = lanes_of(main.shape)
-    return jnp.where(
-        lane < 6, turned(window, -6), jnp.where(lane >= 122, turned(window, 52), main)
-    )
+def short_chain(pressure, wind):
+    for _ in range(SUBSTEPS):
+        after, before = turned(pressure, -1), turned(pressure, 1)
+        old = wind - turned(wind, 1)
+        wind = sub(wind, after - pressure)
+        change = old - COURANT * ((after - pressure) - (pressure - before))
+        pressure = sub(pressure, change)
+    return pressure, wind
 
 
 def odd_tile():
@@ -188,25 +182,71 @@
         part = got_parts(got, peer)
         higher = higher + part
         beyond = beyond + jnp.where(me < peer, 1.0, 0.0) * part
-    to_chip[0:64, :] = raw[...]
-    to_chip[64:72, :] = from_low_half(beyond)
+    border = unfolded(from_low_half(beyond))
+    border = jnp.where(lanes_of(border.shape) < 6, border, 0.0)
+    for shift in (8, 16, 32, 64):
+        border = border + turned(border, shift)
+    to_chip[0:32, :] = raw[0:32, :] + border
+    to_chip[32:64, :] = raw[32:64, :]
 
 
 def slot(level):
     return 32 * (level % 4)
 
 
-def local_substeps(
-    theta, thickness, wind, surface, from_core, out_p, out_w, chip_p, chip_w, core_p, core_w
-):
+def halo_lanes(right):
+    lane = lanes_of((ROWS, LANES)) & 31
+    start = by_side(right, 12, 0)
+    return (lane >= start) & (lane < start + 6)
+
+
+def in_slot(level):
+    lane = lanes_of((ROWS, LANES))
+    return (lane >= slot(level)) & (lane < slot(level) + 32)
+
+
+def band(level):
+    return pl.ds(ROWS * (level // 4), ROWS)
+
+
+def put_halos(base, halos, right, edge, extra):
+    is_halo = halo_lanes(right)
+    for first in range(0, OWN, 4):
+        value = base[band(first), :]
+        for level in range(first, first + 4):
+            here = slot(level)
+            halo = swung(halos, right, here + 12 - 8 * level, here - 8 * level)
+            value = jnp.where(is_halo & in_slot(level), halo, value)
+        edge[band(first), :] = value if extra is None else value + extra
+
+
+def evolve(p, w):
+    p[...], w[...] = short_chain(p[...], w[...])
+
+
+def edge_lanes(right):
+    lane = lanes_of((ROWS, LANES))
+    start = by_side(right, 122, 0)
+    return (lane >= start) & (lane < start + 6)
+
+
+def edge_of(edge, level, right):
+    return swung(edge[band(level), :], right, 116 - slot(level), -6 - slot(level))
+
+
+def in_every_slot(field, right, if_right, if_left, kept):
+    out = None
+    for level in range(4):
+        moved = swung(field, right, slot(level) + if_right, slot(level) + if_left)
+        out = moved if out is None else jnp.where(in_slot(level), moved, out)
+    return jnp.where(kept, out, 0.0)
+
+
+def local_substeps(theta, thickness, wind, surface, out_p, out_w, chip_p, chip_w, core_p, core_w):
     chip_right = odd_tile()
     core_right = jnp.logical_not(chip_right)
-    lane = lanes_of((ROWS, LANES))
     ground = surface[...]
     below = jnp.zeros((ROWS, LANES), F32)
-    halo_from = by_side(core_right, 12, 0)
-    is_halo = ((lane & 31) >= halo_from) & ((lane & 31) < halo_from + 6)
-    halos = [from_core[0:32, :], from_core[32:64, :]]
     packed = None
     for level in reversed(range(OWN)):
         at = pl.ds(level * ROWS, ROWS)
@@ -217,56 +257,53 @@
         here = slot(level)
         if level % 4 == 3:
             packed = [jnp.zeros((ROWS, LANES), F32)] * 4
-        mine = (lane >= here) & (lane < here + 32)
         for i in range(2):
             for j, right in ((0, chip_right), (2, core_right)):
                 side = swung(fields[i], right, here - 116, here + 6)
-                if j == 2:
-                    halo = swung(halos[i], right, here + 12 - 8 * level, here - 8 * level)
-                    side = jnp.where(is_halo, halo, side)
-                packed[i + j] = jnp.where(mine, side, packed[i + j])
+                packed[i + j] = jnp.where(in_slot(level), side, packed[i + j])
         if level % 4 == 0:
-            group = pl.ds(8 * level, ROWS)
             for ref, value in zip((chip_p, chip_w, core_p, core_w), packed):
-                ref[group, :] = value
-    p, w = substeps(out_p[...], wind[...])
-    out_p[...] = p
-    out_w[...] = w
-    p, w = substeps(core_p[...], core_w[...])
-    core_p[...] = p
-    core_w[...] = w
-    fix_edges(out_p, out_w, core_p, core_w, core_right, out_p, out_w, 0.0, 0.0)
-
-
-def fix_edges(base_p, base_w, edge_p, edge_w, right, out_p, out_w, add_p, add_w):
-    lane = lanes_of((ROWS, LANES))
-    start = by_side(right, 122, 0)
-    fixed = (lane >= start) & (lane < start + 6)
-    for level in range(OWN):
-        at = pl.ds(level * ROWS, ROWS)
-        group = pl.ds(ROWS * (level // 4), ROWS)
-        here = slot(level)
-        for base, edge, out, add in (
-            (base_p, edge_p, out_p, add_p),
-            (base_w, edge_w, out_w, add_w),
-        ):
-            moved = swung(edge[group, :], right, 116 - here, -6 - here)
-            out[at, :] = jnp.where(fixed, moved, base[at, :]) + add
-
-
-def spread_heating(got, out_h, out_sum, rows_first):
+                ref[band(level), :] = value
+    out_p[...], out_w[...] = substeps(out_p[...], wind[...])
+
+
+def middle(
+    got, from_core, local_p, local_w, chip_p, core_p, core_w, out_h, out_p, out_w, out_chip, edge_p, edge_w, rows_first
+):
     me = lax.axis_index("lev")
+    chip_right = odd_tile()
+    core_right = jnp.logical_not(chip_right)
     beyond = jnp.zeros((8, LANES), F32)
     pieces = []
     for peer in range(PEERS):
         piece = got_parts(got, peer)
         pieces.append(piece)
         beyond = beyond + jnp.where(me < peer, 1.0, 0.0) * piece
-    for group in range(4):
-        out_sum[8 * group : 8 * group + 8, :] = jnp.where(
-            top_half(), pieces[2 * group], halves_swapped(pieces[2 * group + 1])
-        )
-    out_sum[32:64, :] = unfolded(from_low_half(beyond))
+    higher = jnp.concatenate(
+        [
+            jnp.where(top_half(), pieces[2 * group], halves_swapped(pieces[2 * group + 1]))
+            for group in range(4)
+        ]
+    )
+    border = unfolded(from_low_half(beyond))
+    is_halo = halo_lanes(core_right)
+    extra = in_every_slot(higher, core_right, -116, 6, jnp.logical_not(is_halo))
+    extra = extra + in_every_slot(border, core_right, 12, 0, is_halo)
+    put_halos(core_p, from_core[0:32, :], core_right, edge_p, extra)
+    put_halos(core_w, from_core[32:64, :], core_right, edge_w, None)
+    edge_p[128:160, :] = higher
+    edge_w[128:160, :] = jnp.zeros((ROWS, LANES), F32)
+    evolve(edge_p, edge_w)
+    add_p = edge_p[128:160, :]
+    add_w = edge_w[128:160, :]
+    fixed = edge_lanes(core_right)
+    for level in range(OWN):
+        at = pl.ds(level * ROWS, ROWS)
+        out_p[at, :] = jnp.where(fixed, edge_of(edge_p, level, core_right), local_p[at, :] + add_p)
+        out_w[at, :] = jnp.where(fixed, edge_of(edge_w, level, core_right), local_w[at, :] + add_w)
+    extra = in_every_slot(higher, chip_right, -116, 6, jnp.logical_not(halo_lanes(chip_right)))
+    for first in range(0, OWN, 4):
+        out_chip[band(first), :] = chip_p[band(first), :] + extra
     for peer in range(PEERS):
         rows_first[pl.ds(64 * peer, 64), :] = got[peer, 0:64, :].astype(F32)
     for level in range(OWN):
@@ -275,46 +312,44 @@
         )
 
 
-def finish(from_chip, sums, local_p, local_w, chip_p, chip_w, out_p, out_w, edge_p, edge_w):
+def finish(
+    from_chip, local_p, local_w, chip_p, chip_w, out_p, out_w, edge_p, edge_w, done_p, done_w, sems
+):
     right = odd_tile()
-    lane = lanes_of((ROWS, LANES))
-    halo_from = by_side(right, 12, 0)
-    is_halo = ((lane & 31) >= halo_from) & ((lane & 31) < halo_from + 6)
-    for base, edge, first in ((chip_p, edge_p, 0), (chip_w, edge_w, 32)):
-        halos = from_chip[first : first + 32, :]
-        for group in range(4):
-            at = pl.ds(ROWS * group, ROWS)
-            value = base[at, :]
-            for level in range(4 * group, 4 * group + 4):
-                here = slot(level)
-                mine = is_halo & (lane >= here) & (lane < here + 32)
-                halo = swung(halos, right, here + 12 - 8 * level, here - 8 * level)
-                value = jnp.where(mine, halo, value)
-            edge[at, :] = value
-    p, w = substeps(edge_p[...], edge_w[...])
-    edge_p[...] = p
-    edge_w[...] = w
-    main = sums[0:32, :]
-    core = sums[32:64, :]
-    chip = unfolded(from_chip[64:72, :])
-    side = windowed(
-        main, jnp.where(right, core, chip), turned(jnp.where(right, chip, core), 76)
-    )
-    zero = jnp.zeros((ROWS, LANES), F32)
-    add_p, add_w = substeps(main, zero)
-    side_p, side_w = substeps(side, zero)
-    fix_edges(
-        local_p, local_w, edge_p, edge_w, right, out_p, out_w, edges_in(add_p, side_p), edges_in(add_w, side_w)
-    )
-
-
-def call(kernel, outs, scratch=(), flops=100000, moved=1000000, room=8 << 20):
+    put_halos(chip_p, from_chip[0:32, :], right, edge_p, None)
+    put_halos(chip_w, from_chip[32:64, :], right, edge_w, None)
+    evolve(edge_p, edge_w)
+    fixed = edge_lanes(right)
+    copies = []
+    for first in range(0, OWN, 4):
+        for level in range(first, first + 4):
+            at = pl.ds(level * ROWS, ROWS)
+            done_p[at, :] = jnp.where(fixed, edge_of(edge_p, level, right), local_p[at, :])
+            done_w[at, :] = jnp.where(fixed, edge_of(edge_w, level, right), local_w[at, :])
+        block = pl.ds(first * ROWS, 4 * ROWS)
+        for index, (done, out) in enumerate(((done_p, out_p), (done_w, out_w))):
+            copy = pltpu.make_async_copy(
+                done.at[block, :], out.at[block, :], sems.at[index, first // 4]
+            )
+            copy.start()
+            copies.append(copy)
+    for copy in copies:
+        copy.wait()
+
+
+def call(kernel, outs, scratch=(), flops=100000, moved=1000000, room=8 << 20, own_copies=False):
+    held = [pltpu.VMEM(s, d) for s, d in scratch]
+    more = {}
+    if own_copies:
+        held.append(pltpu.SemaphoreType.DMA((2, 4)))
+        more = dict(out_specs=tuple(pl.BlockSpec(memory_space=pl.ANY) for _ in outs))
     return pl.pallas_call(
         kernel,
         out_shape=tuple(jax.ShapeDtypeStruct(s, d) for s, d in outs),
-        scratch_shapes=[pltpu.VMEM(s, d) for s, d in scratch],
+        scratch_shapes=held,
         compiler_params=pltpu.CompilerParams(vmem_limit_bytes=room),
         cost_estimate=pl.CostEstimate(flops=flops, bytes_accessed=moved, transcendentals=0),
+        **more,
     )
 
 
@@ -331,28 +366,27 @@
     )
     between = [((t + 1) % tiles, (t + 2) % tiles) for t in range(0, tiles, 2)]
     within = [(t, t + 1) for t in range(0, tiles, 2)]
+    packed = (4 * ROWS, LANES)
     from_core = lax.ppermute(to_core, "tile", within + [(b, a) for a, b in within])
+    local_p, local_w, chip_p, chip_w, core_p, core_w = call(
+        local_substeps, [(flat, F32)] * 2 + [(packed, F32)] * 4, flops=20000000
+    )(theta, thickness, wind, surface)
     heats, to_chip = call(
         send_heating,
-        [((PEERS, PIECE, LANES), BF16), ((72, LANES), F32)],
+        [((PEERS, PIECE, LANES), BF16), ((64, LANES), F32)],
         [((512, 512), BF16)],
         flops=70000000,
     )(columns, trigger, closure, closure_weights, from_core, raw)
     heats = lax.all_to_all(heats, "lev", 0, 0, tiled=True)
     from_chip = lax.ppermute(to_chip, "tile", between + [(b, a) for a, b in between])
-    packed = (4 * ROWS, LANES)
-    local_p, local_w, chip_p, chip_w = call(
-        local_substeps,
-        [(flat, F32)] * 2 + [(packed, F32)] * 2,
-        [(packed, F32)] * 2,
-        flops=20000000,
-    )(theta, thickness, wind, surface, from_core)
-    heating, sums = call(
-        spread_heating, [(flat, BF16), ((64, LANES), F32)], [(flat, F32)]
-    )(heats)
-    pressure, wind_next = call(finish, [(flat, F32)] * 2, [(packed, F32)] * 2)(
-        from_chip, sums, local_p, local_w, chip_p, chip_w
-    )
+    heating, local_p, local_w, chip_p = call(
+        middle,
+        [(flat, BF16), (flat, F32), (flat, F32), (packed, F32)],
+        [((5 * ROWS, LANES), F32)] * 2 + [(flat, F32)],
+    )(heats, from_core, local_p, local_w, chip_p, core_p, core_w)
+    pressure, wind_next = call(
+        finish, [(flat, F32)] * 2, [(packed, F32)] * 2 + [(flat, F32)] * 2, own_copies=True
+    )(from_chip, local_p, local_w, chip_p, chip_w)
     shape = (OWN, ROWS, LANES)
     return pressure.reshape(shape), wind_next.reshape(shape), heating.reshape(shape)
 

time: 47.9 us -> 47.7 us (level)
  no operation moved by 1% of the time
where the time goes in v3:
time: 47.7 us; the launch traced here: 47.3 us
  starting transfers between devices  32.4 us (68%)
  Pallas kernels  8.38 us (18%)
  waiting for transfers between devices  5.8 us (12%)
  between operations  0.74 us (2%)
    all_to_all x1, starting transfers between devices, coupled(): columns = lax.all_to_all(columns, 'lev', 0, 0, tiled=True)  16.4 us
    ppermute x1, starting transfers between devices, coupled(): lax.ppermute(to_chip, 'tile', between + [(b, a) for a, b in between])  9.33 us
    all_to_all x1, starting transfers between devices, coupled(): heats = lax.all_to_all(heats, 'lev', 0, 0, tiled=True)  4.74 us
    all_to_all x1, waiting for transfers between devices, coupled(): columns = lax.all_to_all(columns, 'lev', 0, 0, tiled=True)  4.62 us
    pallas_call x1, Pallas kernels, coupled(): call(send_columns, [((PEERS, PIECE, LANES), BF16)], room=60 << 20)  2.07 us
    pallas_call x1, Pallas kernels, coupled(): call(middle, [(flat, BF16), (flat, F32), (flat, F32), (packed, F32)], [((...  1.93 us
    ppermute x1, starting transfers between devices, coupled(): lax.ppermute(to_core, 'tile', within + [(b, a) for a, b in within])  1.92 us
    pallas_call x1, Pallas kernels, coupled(): call(finish, [(flat, F32)] * 2, [(packed, F32)] * 2 + [(flat, F32)] * 2,...  1.71 us
  transfers between devices with their start and end apart: 4, of which 2 were waited for; matrix products, arithmetic and copies ran while one was open for 0% of the time, Pallas kernels for 7%

profile of v3, /device:TPU:16, one launch (start us, length us, event | category | flops | bytes accessed | tf_op | source)
XLA Modules:
  0.0 47.3 jit_solution(18255146243277009133)
XLA Ops:
  0.6 0.0 copy-start.1
  0.6 0.0 copy-start.2
  0.7 2.1 %shard_map.94 = bf16[8,88,128]{2,1,0:T(8,128)(2,1)} custom-call(f32[512,128]{1,0:T(8,128)} %bitcast.6, f32[512,128]{1,0:T(8,128)} %bitcast.9), custom_call_target="tpu_custom_call" | custom-call | flops 100000 | bytes 1000000 | tf_op jit(solution)/shard_map/pallas_call | solution.py:360
  2.7 0.0 copy-start
  2.7 0.0 copy-start.4
  2.7 16.4 %all-to-all-start = ((bf16[8,88,128]{2,1,0:T(8,128)(2,1)}), bf16[8,88,128]{2,1,0:T(8,128)(2,1)S(1)}, u32[]{:S(2)}, u32[]{:S(2)}) async-start(bf16[8,88,128]{2,1,0:T(8,128)(2,1)} %shard_map.94), calls=%async_computation | async-start | bytes 360448 | tf_op jit(solution)/shard_map/all_to_all | solution.py:363
  19.1 0.0 copy-done.1
  19.1 0.0 copy-done.2
  19.1 0.0 copy-done
  19.1 0.0 copy-done.4
  19.1 0.0 copy-start.3
  19.1 0.0 copy-start.5
  19.2 0.0 copy-start.6
  19.2 0.4 shard_map.95
  19.6 1.9 %collective-permute-start = (f32[72,128]{1,0:T(8,128)S(1)}, f32[72,128]{1,0:T(8,128)S(1)}, u32[]{:S(2)}, u32[]{:S(2)}) collective-permute-start(f32[72,128]{1,0:T(8,128)S(1)} %get-tuple-element.19), channel_id=1, source_target_pairs={{0,8},{16,24},{32,40},{48,56},{64,72},{80,88},{96,104},{112,120},{... | collective-permute-start | bytes 110600 | tf_op jit(solution)/shard_map/ppermute | solution.py:370
  21.5 1.2 %collective-permute-done.from_core = f32[72,128]{1,0:T(8,128)S(1)} collective-permute-done((f32[72,128]{1,0:T(8,128)S(1)}, f32[72,128]{1,0:T(8,128)S(1)}, u32[]{:S(2)}, u32[]{:S(2)}) %collective-permute-start) | collective-permute-done | bytes 36896 | tf_op jit(solution)/shard_map/ppermute | solution.py:370
  22.7 4.6 %all-to-all-done.got = bf16[8,88,128]{2,1,0:T(8,128)(2,1)S(1)} async-done(((bf16[8,88,128]{2,1,0:T(8,128)(2,1)}), bf16[8,88,128]{2,1,0:T(8,128)(2,1)S(1)}, u32[]{:S(2)}, u32[]{:S(2)}) %all-to-all-start) | async-done | bytes 180256 | tf_op jit(solution)/shard_map/all_to_all | solution.py:363
  27.3 0.0 copy-done.3
  27.3 0.0 copy-done.5
  27.3 0.0 copy-done.6
  27.3 1.1 %shard_map.96 = (bf16[8,88,128]{2,1,0:T(8,128)(2,1)}, f32[64,128]{1,0:T(8,128)S(1)}) custom-call(bf16[8,88,128]{2,1,0:T(8,128)(2,1)S(1)} %all-to-all-done.got, s32[32,128]{1,0:T(8,128)S(1)} %copy-done.5, s32[32,128]{1,0:T(8,128)S(1)} %copy-done.6, bf16[4,128,128]{2,1,0:T(8,128)(2,1)S(1)} %copy-done.3, f32[72,128]{1,0:T(8,128)S(1)} %collective-permute-done.from_core, ...), custom_call_target="tpu_custom_call" | custom-call | flops 70000000 | bytes 1000000 | tf_op jit(solution)/shard_map/pallas_call | solution.py:374
  28.4 4.7 %all-to-all-start.1 = ((bf16[8,88,128]{2,1,0:T(8,128)(2,1)}), bf16[8,88,128]{2,1,0:T(8,128)(2,1)S(1)}, u32[]{:S(2)}, u32[]{:S(2)}) async-start(bf16[8,88,128]{2,1,0:T(8,128)(2,1)} %get-tuple-element.22), calls=%async_computation.1 | async-start | bytes 360448 | tf_op jit(solution)/shard_map/all_to_all | solution.py:380
  33.1 9.3 %collective-permute-start.1 = (f32[64,128]{1,0:T(8,128)S(1)}, f32[64,128]{1,0:T(8,128)S(1)}, u32[]{:S(2)}, u32[]{:S(2)}) collective-permute-start(f32[64,128]{1,0:T(8,128)S(1)} %get-tuple-element.21), channel_id=1, source_target_pairs={{8,16},{24,32},{40,48},{56,64},{72,80},{88,96},{104,112},{120,128}... | collective-permute-start | bytes 98312 | tf_op jit(solution)/shard_map/ppermute | solution.py:381
  42.5 1.2 %shard_map.97 = (f32[512,128]{1,0:T(8,128)S(1)}, f32[512,128]{1,0:T(8,128)S(1)}, f32[128,128]{1,0:T(8,128)S(1)}, f32[128,128]{1,0:T(8,128)S(1)}, f32[128,128]{1,0:T(8,128)S(1)}, /*index=5*/f32[128,128]{1,0:T(8,128)S(1)}) custom-call(f32[512,128]{1,0:T(8,128)S(1)} %bitcast.8, f32[512,128]{1,0:T(8,128)S(1)} %bitcast.11, f32[512,128]{1,0:T(8,128)S(1)} %bitcast.13, ...), custom_call_target="tpu_custom_call" | custom-call | flops 20000000 | bytes 1000000 | tf_op jit(solution)/shard_map/pallas_call | solution.py:371
  43.7 0.0 all-to-all-done.1.got
  43.7 1.9 %shard_map.98 = (bf16[512,128]{1,0:T(8,128)(2,1)}, f32[512,128]{1,0:T(8,128)S(1)}, f32[512,128]{1,0:T(8,128)S(1)}, f32[128,128]{1,0:T(8,128)S(1)}) custom-call(bf16[8,88,128]{2,1,0:T(8,128)(2,1)S(1)} %all-to-all-done.1.got, f32[72,128]{1,0:T(8,128)S(1)} %collective-permute-done.from_core, f32[512,128]{1,0:T(8,128)S(1)} %get-tuple-element.23.local_p, ...), custom_call_target="tpu_custom_call" | custom-call | flops 100000 | bytes 1000000 | tf_op jit(solution)/shard_map/pallas_call | solution.py:382
  45.6 0.0 collective-permute-done.1.from_chip
  45.6 1.7 %shard_map.99 = (f32[512,128]{1,0:T(8,128)}, f32[512,128]{1,0:T(8,128)}) custom-call(f32[64,128]{1,0:T(8,128)S(1)} %collective-permute-done.1.from_chip, f32[512,128]{1,0:T(8,128)S(1)} %get-tuple-element.28.local_p, f32[512,128]{1,0:T(8,128)S(1)} %get-tuple-element.29.local_w, f32[128,128]{1,0:T(8,128)S(1)} %get-tuple-element.30.chip_p, ...), custom_call_target="tpu_custom_call" | custom-call | flops 100000 | bytes 1000000 | tf_op jit(solution)/shard_map/pallas_call | solution.py:387
Async XLA Ops:
  0.6 18.5 %copy-start.1 = (f32[16,32,128]{2,1,0:T(8,128)S(1)}, f32[16,32,128]{2,1,0:T(8,128)}, u32[]{:S(2)}) copy-start(f32[16,32,128]{2,1,0:T(8,128)} %param.8) | copy-start | bytes 786436
  0.6 18.5 %copy-start.2 = (f32[16,32,128]{2,1,0:T(8,128)S(1)}, f32[16,32,128]{2,1,0:T(8,128)}, u32[]{:S(2)}) copy-start(f32[16,32,128]{2,1,0:T(8,128)} %param.9) | copy-start | bytes 786436
  2.7 16.4 %copy-start = (f32[16,32,128]{2,1,0:T(8,128)S(1)}, f32[16,32,128]{2,1,0:T(8,128)}, u32[]{:S(2)}) copy-start(f32[16,32,128]{2,1,0:T(8,128)} %param.7) | copy-start | bytes 786436
  2.7 16.4 %copy-start.4 = (f32[32,128]{1,0:T(8,128)S(1)}, f32[32,128]{1,0:T(8,128)}, u32[]{:S(2)}) copy-start(f32[32,128]{1,0:T(8,128)} %surface.3) | copy-start | bytes 49156
  2.7 24.6 %all-to-all-start = ((bf16[8,88,128]{2,1,0:T(8,128)(2,1)}), bf16[8,88,128]{2,1,0:T(8,128)(2,1)S(1)}, u32[]{:S(2)}, u32[]{:S(2)}) async-start(bf16[8,88,128]{2,1,0:T(8,128)(2,1)} %shard_map.94), calls=%async_computation | async-start | bytes 360448 | tf_op jit(solution)/shard_map/all_to_all | solution.py:363
  19.1 8.1 %copy-start.3 = (bf16[4,128,128]{2,1,0:T(8,128)(2,1)S(1)}, bf16[4,128,128]{2,1,0:T(8,128)(2,1)}, u32[]{:S(2)}) copy-start(bf16[4,128,128]{2,1,0:T(8,128)(2,1)} %weights.1) | copy-start | bytes 393220
  19.1 8.1 %copy-start.5 = (s32[32,128]{1,0:T(8,128)S(1)}, s32[32,128]{1,0:T(8,128)}, u32[]{:S(2)}) copy-start(s32[32,128]{1,0:T(8,128)} %trigger.1) | copy-start | bytes 49156
  19.2 8.1 %copy-start.6 = (s32[32,128]{1,0:T(8,128)S(1)}, s32[32,128]{1,0:T(8,128)}, u32[]{:S(2)}) copy-start(s32[32,128]{1,0:T(8,128)} %closure.1) | copy-start | bytes 49156
  19.6 3.1 %collective-permute-start = (f32[72,128]{1,0:T(8,128)S(1)}, f32[72,128]{1,0:T(8,128)S(1)}, u32[]{:S(2)}, u32[]{:S(2)}) collective-permute-start(f32[72,128]{1,0:T(8,128)S(1)} %get-tuple-element.19), channel_id=1, source_target_pairs={{0,8},{16,24},{32,40},{48,56},{64,72},{80,88},{96,104},{112,120},{... | collective-permute-start | bytes 110600 | tf_op jit(solution)/shard_map/ppermute | solution.py:370
  28.4 15.3 %all-to-all-start.1 = ((bf16[8,88,128]{2,1,0:T(8,128)(2,1)}), bf16[8,88,128]{2,1,0:T(8,128)(2,1)S(1)}, u32[]{:S(2)}, u32[]{:S(2)}) async-start(bf16[8,88,128]{2,1,0:T(8,128)(2,1)} %get-tuple-element.22), calls=%async_computation.1 | async-start | bytes 360448 | tf_op jit(solution)/shard_map/all_to_all | solution.py:380
  33.1 12.5 %collective-permute-start.1 = (f32[64,128]{1,0:T(8,128)S(1)}, f32[64,128]{1,0:T(8,128)S(1)}, u32[]{:S(2)}, u32[]{:S(2)}) collective-permute-start(f32[64,128]{1,0:T(8,128)S(1)} %get-tuple-element.21), channel_id=1, source_target_pairs={{8,16},{24,32},{40,48},{56,64},{72,80},{88,96},{104,112},{120,128}... | collective-permute-start | bytes 98312 | tf_op jit(solution)/shard_map/ppermute | solution.py:381

commit v4 on v3

--- a/solution.py
+++ b/solution.py
@@ -45,18 +45,10 @@
 
 def substeps(pressure, wind):
     for _ in range(SUBSTEPS):
-        wind = sub(wind, turned(pressure, -1) - pressure)
-        pressure = sub(pressure, wind - turned(wind, 1))
-    return pressure, wind
-
-
-def short_chain(pressure, wind):
-    for _ in range(SUBSTEPS):
-        after, before = turned(pressure, -1), turned(pressure, 1)
-        old = wind - turned(wind, 1)
+        after = turned(pressure, -1)
+        before = turned(wind + COURANT * pressure, 1) - COURANT * pressure
         wind = sub(wind, after - pressure)
-        change = old - COURANT * ((after - pressure) - (pressure - before))
-        pressure = sub(pressure, change)
+        pressure = sub(pressure, wind - before)
     return pressure, wind
 
 
@@ -221,7 +213,7 @@
 
 
 def evolve(p, w):
-    p[...], w[...] = short_chain(p[...], w[...])
+    p[...], w[...] = substeps(p[...], w[...])
 
 
 def edge_lanes(right):
@@ -313,14 +305,15 @@
 
 
 def finish(
-    from_chip, local_p, local_w, chip_p, chip_w, out_p, out_w, edge_p, edge_w, done_p, done_w, sems
+    from_chip, heating, local_p, local_w, chip_p, chip_w, out_p, out_w, out_h, edge_p, edge_w, done_p, done_w, sems
 ):
+    copies = [pltpu.make_async_copy(heating, out_h, sems.at[8])]
+    copies[0].start()
     right = odd_tile()
     put_halos(chip_p, from_chip[0:32, :], right, edge_p, None)
     put_halos(chip_w, from_chip[32:64, :], right, edge_w, None)
     evolve(edge_p, edge_w)
     fixed = edge_lanes(right)
-    copies = []
     for first in range(0, OWN, 4):
         for level in range(first, first + 4):
             at = pl.ds(level * ROWS, ROWS)
@@ -329,7 +322,7 @@
         block = pl.ds(first * ROWS, 4 * ROWS)
         for index, (done, out) in enumerate(((done_p, out_p), (done_w, out_w))):
             copy = pltpu.make_async_copy(
-                done.at[block, :], out.at[block, :], sems.at[index, first // 4]
+                done.at[block, :], out.at[block, :], sems.at[4 * index + first // 4]
             )
             copy.start()
             copies.append(copy)
@@ -341,7 +334,7 @@
     held = [pltpu.VMEM(s, d) for s, d in scratch]
     more = {}
     if own_copies:
-        held.append(pltpu.SemaphoreType.DMA((2, 4)))
+        held.append(pltpu.SemaphoreType.DMA((9,)))
         more = dict(out_specs=tuple(pl.BlockSpec(memory_space=pl.ANY) for _ in outs))
     return pl.pallas_call(
         kernel,
@@ -384,9 +377,12 @@
         [(flat, BF16), (flat, F32), (flat, F32), (packed, F32)],
         [((5 * ROWS, LANES), F32)] * 2 + [(flat, F32)],
     )(heats, from_core, local_p, local_w, chip_p, core_p, core_w)
-    pressure, wind_next = call(
-        finish, [(flat, F32)] * 2, [(packed, F32)] * 2 + [(flat, F32)] * 2, own_copies=True
-    )(from_chip, local_p, local_w, chip_p, chip_w)
+    pressure, wind_next, heating = call(
+        finish,
+        [(flat, F32), (flat, F32), (flat, BF16)],
+        [(packed, F32)] * 2 + [(flat, F32)] * 2,
+        own_copies=True,
+    )(from_chip, heating, local_p, local_w, chip_p, chip_w)
     shape = (OWN, ROWS, LANES)
     return pressure.reshape(shape), wind_next.reshape(shape), heating.reshape(shape)
 

time: 47.7 us -> 47.1 us (0.987)
  Pallas kernels: 8.38 us -> 7.71 us
    pallas_call x1, Pallas kernels: 1.93 us -> 1.24 us  [coupled(): call(middle, [(flat, BF16), (flat, F32), (flat, F32), (packed, F32)], [((...]
  transfers between devices with their start and end apart: 4 -> 4, of which waited for: 2 -> 2; matrix products, arithmetic and copies ran while one was open for 0% -> 0% of each run, Pallas kernels for 7% -> 6%
where the time goes in v4:
time: 47.1 us; the launch traced here: 46.7 us
  starting transfers between devices  32.4 us (69%)
  Pallas kernels  7.71 us (16%)
  waiting for transfers between devices  5.8 us (12%)
  between operations  0.75 us (2%)
    all_to_all x1, starting transfers between devices, coupled(): columns = lax.all_to_all(columns, 'lev', 0, 0, tiled=True)  16.4 us
    ppermute x1, starting transfers between devices, coupled(): lax.ppermute(to_chip, 'tile', between + [(b, a) for a, b in between])  9.33 us
    all_to_all x1, starting transfers between devices, coupled(): heats = lax.all_to_all(heats, 'lev', 0, 0, tiled=True)  4.74 us
    all_to_all x1, waiting for transfers between devices, coupled(): columns = lax.all_to_all(columns, 'lev', 0, 0, tiled=True)  4.62 us
    pallas_call x1, Pallas kernels, coupled(): call(send_columns, [((PEERS, PIECE, LANES), BF16)], room=60 << 20)  2.07 us
    ppermute x1, starting transfers between devices, coupled(): lax.ppermute(to_core, 'tile', within + [(b, a) for a, b in within])  1.92 us
    pallas_call x1, Pallas kernels, coupled(): call(finish, [(flat, F32), (flat, F32), (flat, BF16)], [(packed, F32)] *...  1.71 us
    pallas_call x1, Pallas kernels, coupled(): call(local_substeps, [(flat, F32)] * 2 + [(packed, F32)] * 4, flops=20000...  1.24 us
  transfers between devices with their start and end apart: 4, of which 2 were waited for; matrix products, arithmetic and copies ran while one was open for 0% of the time, Pallas kernels for 6%

profile of v4, /device:TPU:16, one launch (start us, length us, event | category | flops | bytes accessed | tf_op | source)
XLA Modules:
  0.0 46.7 jit_solution(17369190041586552520)
XLA Ops:
  0.6 0.0 copy-start.1
  0.6 0.0 copy-start.2
  0.7 2.1 %shard_map.94 = bf16[8,88,128]{2,1,0:T(8,128)(2,1)} custom-call(f32[512,128]{1,0:T(8,128)} %bitcast.6, f32[512,128]{1,0:T(8,128)} %bitcast.9), custom_call_target="tpu_custom_call" | custom-call | flops 100000 | bytes 1000000 | tf_op jit(solution)/shard_map/pallas_call | solution.py:353
  2.7 0.0 copy-start
  2.7 0.0 copy-start.4
  2.7 16.4 %all-to-all-start = ((bf16[8,88,128]{2,1,0:T(8,128)(2,1)}), bf16[8,88,128]{2,1,0:T(8,128)(2,1)S(1)}, u32[]{:S(2)}, u32[]{:S(2)}) async-start(bf16[8,88,128]{2,1,0:T(8,128)(2,1)} %shard_map.94), calls=%async_computation | async-start | bytes 360448 | tf_op jit(solution)/shard_map/all_to_all | solution.py:356
  19.1 0.0 copy-done.1
  19.1 0.0 copy-done.2
  19.1 0.0 copy-done
  19.1 0.0 copy-done.4
  19.1 0.0 copy-start.3
  19.1 0.0 copy-start.5
  19.2 0.0 copy-start.6
  19.2 0.4 shard_map.95
  19.6 1.9 %collective-permute-start = (f32[72,128]{1,0:T(8,128)S(1)}, f32[72,128]{1,0:T(8,128)S(1)}, u32[]{:S(2)}, u32[]{:S(2)}) collective-permute-start(f32[72,128]{1,0:T(8,128)S(1)} %get-tuple-element.20), channel_id=1, source_target_pairs={{0,8},{16,24},{32,40},{48,56},{64,72},{80,88},{96,104},{112,120},{... | collective-permute-start | bytes 110600 | tf_op jit(solution)/shard_map/ppermute | solution.py:363
  21.5 1.2 %collective-permute-done.from_core = f32[72,128]{1,0:T(8,128)S(1)} collective-permute-done((f32[72,128]{1,0:T(8,128)S(1)}, f32[72,128]{1,0:T(8,128)S(1)}, u32[]{:S(2)}, u32[]{:S(2)}) %collective-permute-start) | collective-permute-done | bytes 36896 | tf_op jit(solution)/shard_map/ppermute | solution.py:363
  22.7 4.6 %all-to-all-done.got = bf16[8,88,128]{2,1,0:T(8,128)(2,1)S(1)} async-done(((bf16[8,88,128]{2,1,0:T(8,128)(2,1)}), bf16[8,88,128]{2,1,0:T(8,128)(2,1)S(1)}, u32[]{:S(2)}, u32[]{:S(2)}) %all-to-all-start) | async-done | bytes 180256 | tf_op jit(solution)/shard_map/all_to_all | solution.py:356
  27.3 0.0 copy-done.3
  27.3 0.0 copy-done.5
  27.3 0.0 copy-done.6
  27.3 1.1 %shard_map.96 = (bf16[8,88,128]{2,1,0:T(8,128)(2,1)}, f32[64,128]{1,0:T(8,128)S(1)}) custom-call(bf16[8,88,128]{2,1,0:T(8,128)(2,1)S(1)} %all-to-all-done.got, s32[32,128]{1,0:T(8,128)S(1)} %copy-done.5, s32[32,128]{1,0:T(8,128)S(1)} %copy-done.6, bf16[4,128,128]{2,1,0:T(8,128)(2,1)S(1)} %copy-done.3, f32[72,128]{1,0:T(8,128)S(1)} %collective-permute-done.from_core, ...), custom_call_target="tpu_custom_call" | custom-call | flops 70000000 | bytes 1000000 | tf_op jit(solution)/shard_map/pallas_call | solution.py:367
  28.4 4.7 %all-to-all-start.1 = ((bf16[8,88,128]{2,1,0:T(8,128)(2,1)}), bf16[8,88,128]{2,1,0:T(8,128)(2,1)S(1)}, u32[]{:S(2)}, u32[]{:S(2)}) async-start(bf16[8,88,128]{2,1,0:T(8,128)(2,1)} %get-tuple-element.23), calls=%async_computation.1 | async-start | bytes 360448 | tf_op jit(solution)/shard_map/all_to_all | solution.py:373
  33.1 9.3 %collective-permute-start.1 = (f32[64,128]{1,0:T(8,128)S(1)}, f32[64,128]{1,0:T(8,128)S(1)}, u32[]{:S(2)}, u32[]{:S(2)}) collective-permute-start(f32[64,128]{1,0:T(8,128)S(1)} %get-tuple-element.22), channel_id=1, source_target_pairs={{8,16},{24,32},{40,48},{56,64},{72,80},{88,96},{104,112},{120,128}... | collective-permute-start | bytes 98312 | tf_op jit(solution)/shard_map/ppermute | solution.py:374
  42.5 1.2 %shard_map.97 = (f32[512,128]{1,0:T(8,128)S(1)}, f32[512,128]{1,0:T(8,128)S(1)}, f32[128,128]{1,0:T(8,128)S(1)}, f32[128,128]{1,0:T(8,128)S(1)}, f32[128,128]{1,0:T(8,128)S(1)}, /*index=5*/f32[128,128]{1,0:T(8,128)S(1)}) custom-call(f32[512,128]{1,0:T(8,128)S(1)} %bitcast.8, f32[512,128]{1,0:T(8,128)S(1)} %bitcast.11, f32[512,128]{1,0:T(8,128)S(1)} %bitcast.13, ...), custom_call_target="tpu_custom_call" | custom-call | flops 20000000 | bytes 1000000 | tf_op jit(solution)/shard_map/pallas_call | solution.py:364
  43.7 0.0 all-to-all-done.1.got
  43.7 1.2 %shard_map.98 = (bf16[512,128]{1,0:T(8,128)(2,1)S(1)}, f32[512,128]{1,0:T(8,128)S(1)}, f32[512,128]{1,0:T(8,128)S(1)}, f32[128,128]{1,0:T(8,128)S(1)}) custom-call(bf16[8,88,128]{2,1,0:T(8,128)(2,1)S(1)} %all-to-all-done.1.got, f32[72,128]{1,0:T(8,128)S(1)} %collective-permute-done.from_core, f32[512,128]{1,0:T(8,128)S(1)} %get-tuple-element.24.local_p, ...), custom_call_target="tpu_custom_call" | custom-call | flops 100000 | bytes 1000000 | tf_op jit(solution)/shard_map/pallas_call | solution.py:375
  45.0 0.0 collective-permute-done.1.from_chip
  45.0 1.7 %shard_map.99 = (f32[512,128]{1,0:T(8,128)}, f32[512,128]{1,0:T(8,128)}, bf16[512,128]{1,0:T(8,128)(2,1)}) custom-call(f32[64,128]{1,0:T(8,128)S(1)} %collective-permute-done.1.from_chip, bf16[512,128]{1,0:T(8,128)(2,1)S(1)} %get-tuple-element.29.heating, f32[512,128]{1,0:T(8,128)S(1)} %get-tuple-element.30.local_p, ...), custom_call_target="tpu_custom_call" | custom-call | flops 100000 | bytes 1000000 | tf_op jit(solution)/shard_map/pallas_call | solution.py:380
Async XLA Ops:
  0.6 18.5 %copy-start.1 = (f32[16,32,128]{2,1,0:T(8,128)S(1)}, f32[16,32,128]{2,1,0:T(8,128)}, u32[]{:S(2)}) copy-start(f32[16,32,128]{2,1,0:T(8,128)} %param.8) | copy-start | bytes 786436
  0.6 18.5 %copy-start.2 = (f32[16,32,128]{2,1,0:T(8,128)S(1)}, f32[16,32,128]{2,1,0:T(8,128)}, u32[]{:S(2)}) copy-start(f32[16,32,128]{2,1,0:T(8,128)} %param.9) | copy-start | bytes 786436
  2.7 16.4 %copy-start = (f32[16,32,128]{2,1,0:T(8,128)S(1)}, f32[16,32,128]{2,1,0:T(8,128)}, u32[]{:S(2)}) copy-start(f32[16,32,128]{2,1,0:T(8,128)} %param.7) | copy-start | bytes 786436
  2.7 16.4 %copy-start.4 = (f32[32,128]{1,0:T(8,128)S(1)}, f32[32,128]{1,0:T(8,128)}, u32[]{:S(2)}) copy-start(f32[32,128]{1,0:T(8,128)} %surface.3) | copy-start | bytes 49156
  2.7 24.6 %all-to-all-start = ((bf16[8,88,128]{2,1,0:T(8,128)(2,1)}), bf16[8,88,128]{2,1,0:T(8,128)(2,1)S(1)}, u32[]{:S(2)}, u32[]{:S(2)}) async-start(bf16[8,88,128]{2,1,0:T(8,128)(2,1)} %shard_map.94), calls=%async_computation | async-start | bytes 360448 | tf_op jit(solution)/shard_map/all_to_all | solution.py:356
  19.1 8.1 %copy-start.3 = (bf16[4,128,128]{2,1,0:T(8,128)(2,1)S(1)}, bf16[4,128,128]{2,1,0:T(8,128)(2,1)}, u32[]{:S(2)}) copy-start(bf16[4,128,128]{2,1,0:T(8,128)(2,1)} %weights.1) | copy-start | bytes 393220
  19.1 8.1 %copy-start.5 = (s32[32,128]{1,0:T(8,128)S(1)}, s32[32,128]{1,0:T(8,128)}, u32[]{:S(2)}) copy-start(s32[32,128]{1,0:T(8,128)} %trigger.1) | copy-start | bytes 49156
  19.2 8.1 %copy-start.6 = (s32[32,128]{1,0:T(8,128)S(1)}, s32[32,128]{1,0:T(8,128)}, u32[]{:S(2)}) copy-start(s32[32,128]{1,0:T(8,128)} %closure.1) | copy-start | bytes 49156
  19.6 3.1 %collective-permute-start = (f32[72,128]{1,0:T(8,128)S(1)}, f32[72,128]{1,0:T(8,128)S(1)}, u32[]{:S(2)}, u32[]{:S(2)}) collective-permute-start(f32[72,128]{1,0:T(8,128)S(1)} %get-tuple-element.20), channel_id=1, source_target_pairs={{0,8},{16,24},{32,40},{48,56},{64,72},{80,88},{96,104},{112,120},{... | collective-permute-start | bytes 110600 | tf_op jit(solution)/shard_map/ppermute | solution.py:363
  28.4 15.3 %all-to-all-start.1 = ((bf16[8,88,128]{2,1,0:T(8,128)(2,1)}), bf16[8,88,128]{2,1,0:T(8,128)(2,1)S(1)}, u32[]{:S(2)}, u32[]{:S(2)}) async-start(bf16[8,88,128]{2,1,0:T(8,128)(2,1)} %get-tuple-element.23), calls=%async_computation.1 | async-start | bytes 360448 | tf_op jit(solution)/shard_map/all_to_all | solution.py:373
  33.1 11.8 %collective-permute-start.1 = (f32[64,128]{1,0:T(8,128)S(1)}, f32[64,128]{1,0:T(8,128)S(1)}, u32[]{:S(2)}, u32[]{:S(2)}) collective-permute-start(f32[64,128]{1,0:T(8,128)S(1)} %get-tuple-element.22), channel_id=1, source_target_pairs={{8,16},{24,32},{40,48},{56,64},{72,80},{88,96},{104,112},{120,128}... | collective-permute-start | bytes 98312 | tf_op jit(solution)/shard_map/ppermute | solution.py:374

commit v5 on v4

--- a/solution.py
+++ b/solution.py
@@ -104,6 +104,21 @@
     return (pair[0:8] + pair[8:16]) + got[peer, 80:88, :].astype(F32)
 
 
+def in_two_rows(fold):
+    rows = [turned(pltpu.roll(fold, 8 - 2 * pair, 0), 32 * pair) for pair in range(1, 4)]
+    return ((fold + rows[0]) + rows[1]) + rows[2]
+
+
+def from_two_rows(packed):
+    row = rows_of(packed.shape)
+    out = packed
+    for pair in range(1, 4):
+        out = jnp.where(
+            row >= 2 * pair, turned(pltpu.roll(packed, 2 * pair, 0), -32 * pair), out
+        )
+    return out
+
+
 def send_columns(theta, thickness, out):
     total = jnp.zeros((ROWS, LANES), F32)
     for level in range(OWN):
@@ -112,11 +127,16 @@
     for row in range(ROWS):
         picked = theta[pl.ds(row, OWN, stride=ROWS), :]
         out[row // BAND, pl.ds(OWN * (row % BAND), OWN), :] = picked.astype(BF16)
-    border = in_low_half(folded(swung(total, odd_tile(), -122, 0)))
+    high, middle, _ = three_parts(in_two_rows(folded(swung(total, odd_tile(), -122, 0))))
+    row = rows_of((8, LANES))
+    border = jnp.where(row < 6, halves_swapped(high), pltpu.roll(middle, 6, 0))
     for group in range(4):
-        rows = total[8 * group : 8 * group + 8]
-        send_parts(out, 2 * group, jnp.where(top_half(), rows, border))
-        send_parts(out, 2 * group + 1, jnp.where(top_half(), halves_swapped(rows), border))
+        parts = three_parts(total[8 * group : 8 * group + 8])
+        for side in range(2):
+            same = [p if side == 0 else halves_swapped(p) for p in parts]
+            first = jnp.where(top_half(), same[0], halves_swapped(same[1]))
+            second = jnp.where(top_half(), same[2], border)
+            out[2 * group + side, 64:80, :] = jnp.concatenate([first, second]).astype(BF16)
 
 
 def send_borders(theta, thickness, wind, surface, to_chip, to_core):
@@ -171,10 +191,11 @@
     beyond = jnp.zeros((8, LANES), F32)
     for peer in reversed(range(PEERS)):
         send_parts(out, peer, jnp.where(top_half(), higher, core_border))
-        part = got_parts(got, peer)
-        higher = higher + part
+        pair = got[peer, 64:80, :].astype(F32)
+        higher = higher + ((pair[0:8] + halves_swapped(pair[0:8])) + pair[8:16])
+        part = halves_swapped(pair[8:16]) + pltpu.roll(pair[8:16], 2, 0)
         beyond = beyond + jnp.where(me < peer, 1.0, 0.0) * part
-    border = unfolded(from_low_half(beyond))
+    border = unfolded(from_two_rows(beyond))
     border = jnp.where(lanes_of(border.shape) < 6, border, 0.0)
     for shift in (8, 16, 32, 64):
         border = border + turned(border, shift)
@@ -350,7 +371,7 @@
     flat = (OWN * ROWS, LANES)
     theta, thickness, wind = (x.reshape(flat) for x in (theta, thickness, wind))
     tiles = lax.axis_size("tile")
-    (columns,) = call(send_columns, [((PEERS, PIECE, LANES), BF16)], room=60 << 20)(
+    (columns,) = call(send_columns, [((PEERS, 80, LANES), BF16)], room=60 << 20)(
         theta, thickness
     )
     columns = lax.all_to_all(columns, "lev", 0, 0, tiled=True)

time: 47.1 us -> 46.6 us (0.989)
  no operation moved by 1% of the time
where the time goes in v5:
time: 46.6 us; the launch traced here: 46.2 us
  starting transfers between devices  32.1 us (69%)
  Pallas kernels  7.71 us (17%)
  waiting for transfers between devices  5.63 us (12%)
  between operations  0.75 us (2%)
    all_to_all x1, starting transfers between devices, coupled(): columns = lax.all_to_all(columns, 'lev', 0, 0, tiled=True)  16.4 us
    ppermute x1, starting transfers between devices, coupled(): lax.ppermute(to_chip, 'tile', between + [(b, a) for a, b in between])  9.03 us
    all_to_all x1, starting transfers between devices, coupled(): heats = lax.all_to_all(heats, 'lev', 0, 0, tiled=True)  4.75 us
    all_to_all x1, waiting for transfers between devices, coupled(): columns = lax.all_to_all(columns, 'lev', 0, 0, tiled=True)  4.44 us
    pallas_call x1, Pallas kernels, coupled(): call(send_columns, [((PEERS, 80, LANES), BF16)], room=60 << 20)  2.05 us
    ppermute x1, starting transfers between devices, coupled(): lax.ppermute(to_core, 'tile', within + [(b, a) for a, b in within])  1.92 us
    pallas_call x1, Pallas kernels, coupled(): call(finish, [(flat, F32), (flat, F32), (flat, BF16)], [(packed, F32)] *...  1.71 us
    pallas_call x1, Pallas kernels, coupled(): call(local_substeps, [(flat, F32)] * 2 + [(packed, F32)] * 4, flops=20000...  1.24 us
  transfers between devices with their start and end apart: 4, of which 2 were waited for; matrix products, arithmetic and copies ran while one was open for 0% of the time, Pallas kernels for 6%

profile of v5, /device:TPU:16, one launch (start us, length us, event | category | flops | bytes accessed | tf_op | source)
XLA Modules:
  0.0 46.2 jit_solution(14735493441688898209)
XLA Ops:
  0.6 0.0 copy-start.1
  0.6 0.0 copy-start.2
  0.7 2.1 %shard_map.94 = bf16[8,80,128]{2,1,0:T(8,128)(2,1)} custom-call(f32[512,128]{1,0:T(8,128)} %bitcast.6, f32[512,128]{1,0:T(8,128)} %bitcast.9), custom_call_target="tpu_custom_call" | custom-call | flops 100000 | bytes 1000000 | tf_op jit(solution)/shard_map/pallas_call | solution.py:374
  2.7 0.0 copy-start
  2.7 0.0 copy-start.4
  2.7 16.4 %all-to-all-start = ((bf16[8,80,128]{2,1,0:T(8,128)(2,1)}), bf16[8,80,128]{2,1,0:T(8,128)(2,1)S(1)}, u32[]{:S(2)}, u32[]{:S(2)}) async-start(bf16[8,80,128]{2,1,0:T(8,128)(2,1)} %shard_map.94), calls=%async_computation | async-start | bytes 327680 | tf_op jit(solution)/shard_map/all_to_all | solution.py:377
  19.1 0.0 copy-done.1
  19.1 0.0 copy-done.2
  19.1 0.0 copy-done
  19.1 0.0 copy-done.4
  19.1 0.0 copy-start.3
  19.1 0.0 copy-start.5
  19.1 0.0 copy-start.6
  19.1 0.4 shard_map.95
  19.5 1.9 %collective-permute-start = (f32[72,128]{1,0:T(8,128)S(1)}, f32[72,128]{1,0:T(8,128)S(1)}, u32[]{:S(2)}, u32[]{:S(2)}) collective-permute-start(f32[72,128]{1,0:T(8,128)S(1)} %get-tuple-element.20), channel_id=1, source_target_pairs={{0,8},{16,24},{32,40},{48,56},{64,72},{80,88},{96,104},{112,120},{... | collective-permute-start | bytes 110600 | tf_op jit(solution)/shard_map/ppermute | solution.py:384
  21.5 1.2 %collective-permute-done.from_core = f32[72,128]{1,0:T(8,128)S(1)} collective-permute-done((f32[72,128]{1,0:T(8,128)S(1)}, f32[72,128]{1,0:T(8,128)S(1)}, u32[]{:S(2)}, u32[]{:S(2)}) %collective-permute-start) | collective-permute-done | bytes 36896 | tf_op jit(solution)/shard_map/ppermute | solution.py:384
  22.6 4.4 %all-to-all-done.got = bf16[8,80,128]{2,1,0:T(8,128)(2,1)S(1)} async-done(((bf16[8,80,128]{2,1,0:T(8,128)(2,1)}), bf16[8,80,128]{2,1,0:T(8,128)(2,1)S(1)}, u32[]{:S(2)}, u32[]{:S(2)}) %all-to-all-start) | async-done | bytes 163872 | tf_op jit(solution)/shard_map/all_to_all | solution.py:377
  27.1 0.0 copy-done.3
  27.1 0.0 copy-done.5
  27.1 0.0 copy-done.6
  27.1 1.1 %shard_map.96 = (bf16[8,88,128]{2,1,0:T(8,128)(2,1)}, f32[64,128]{1,0:T(8,128)S(1)}) custom-call(bf16[8,80,128]{2,1,0:T(8,128)(2,1)S(1)} %all-to-all-done.got, s32[32,128]{1,0:T(8,128)S(1)} %copy-done.5, s32[32,128]{1,0:T(8,128)S(1)} %copy-done.6, bf16[4,128,128]{2,1,0:T(8,128)(2,1)S(1)} %copy-done.3, f32[72,128]{1,0:T(8,128)S(1)} %collective-permute-done.from_core, ...), custom_call_target="tpu_custom_call" | custom-call | flops 70000000 | bytes 1000000 | tf_op jit(solution)/shard_map/pallas_call | solution.py:388
  28.2 4.7 %all-to-all-start.1 = ((bf16[8,88,128]{2,1,0:T(8,128)(2,1)}), bf16[8,88,128]{2,1,0:T(8,128)(2,1)S(1)}, u32[]{:S(2)}, u32[]{:S(2)}) async-start(bf16[8,88,128]{2,1,0:T(8,128)(2,1)} %get-tuple-element.23), calls=%async_computation.1 | async-start | bytes 360448 | tf_op jit(solution)/shard_map/all_to_all | solution.py:394
  32.9 9.0 %collective-permute-start.1 = (f32[64,128]{1,0:T(8,128)S(1)}, f32[64,128]{1,0:T(8,128)S(1)}, u32[]{:S(2)}, u32[]{:S(2)}) collective-permute-start(f32[64,128]{1,0:T(8,128)S(1)} %get-tuple-element.22), channel_id=1, source_target_pairs={{8,16},{24,32},{40,48},{56,64},{72,80},{88,96},{104,112},{120,128}... | collective-permute-start | bytes 98312 | tf_op jit(solution)/shard_map/ppermute | solution.py:395
  42.0 1.2 %shard_map.97 = (f32[512,128]{1,0:T(8,128)S(1)}, f32[512,128]{1,0:T(8,128)S(1)}, f32[128,128]{1,0:T(8,128)S(1)}, f32[128,128]{1,0:T(8,128)S(1)}, f32[128,128]{1,0:T(8,128)S(1)}, /*index=5*/f32[128,128]{1,0:T(8,128)S(1)}) custom-call(f32[512,128]{1,0:T(8,128)S(1)} %bitcast.8, f32[512,128]{1,0:T(8,128)S(1)} %bitcast.11, f32[512,128]{1,0:T(8,128)S(1)} %bitcast.13, ...), custom_call_target="tpu_custom_call" | custom-call | flops 20000000 | bytes 1000000 | tf_op jit(solution)/shard_map/pallas_call | solution.py:385
  43.2 0.0 all-to-all-done.1.got
  43.2 1.2 %shard_map.98 = (bf16[512,128]{1,0:T(8,128)(2,1)S(1)}, f32[512,128]{1,0:T(8,128)S(1)}, f32[512,128]{1,0:T(8,128)S(1)}, f32[128,128]{1,0:T(8,128)S(1)}) custom-call(bf16[8,88,128]{2,1,0:T(8,128)(2,1)S(1)} %all-to-all-done.1.got, f32[72,128]{1,0:T(8,128)S(1)} %collective-permute-done.from_core, f32[512,128]{1,0:T(8,128)S(1)} %get-tuple-element.24.local_p, ...), custom_call_target="tpu_custom_call" | custom-call | flops 100000 | bytes 1000000 | tf_op jit(solution)/shard_map/pallas_call | solution.py:396
  44.5 0.0 collective-permute-done.1.from_chip
  44.5 1.7 %shard_map.99 = (f32[512,128]{1,0:T(8,128)}, f32[512,128]{1,0:T(8,128)}, bf16[512,128]{1,0:T(8,128)(2,1)}) custom-call(f32[64,128]{1,0:T(8,128)S(1)} %collective-permute-done.1.from_chip, bf16[512,128]{1,0:T(8,128)(2,1)S(1)} %get-tuple-element.29.heating, f32[512,128]{1,0:T(8,128)S(1)} %get-tuple-element.30.local_p, ...), custom_call_target="tpu_custom_call" | custom-call | flops 100000 | bytes 1000000 | tf_op jit(solution)/shard_map/pallas_call | solution.py:401
Async XLA Ops:
  0.6 18.5 %copy-start.1 = (f32[16,32,128]{2,1,0:T(8,128)S(1)}, f32[16,32,128]{2,1,0:T(8,128)}, u32[]{:S(2)}) copy-start(f32[16,32,128]{2,1,0:T(8,128)} %param.8) | copy-start | bytes 786436
  0.6 18.4 %copy-start.2 = (f32[16,32,128]{2,1,0:T(8,128)S(1)}, f32[16,32,128]{2,1,0:T(8,128)}, u32[]{:S(2)}) copy-start(f32[16,32,128]{2,1,0:T(8,128)} %param.9) | copy-start | bytes 786436
  2.7 16.4 %copy-start = (f32[16,32,128]{2,1,0:T(8,128)S(1)}, f32[16,32,128]{2,1,0:T(8,128)}, u32[]{:S(2)}) copy-start(f32[16,32,128]{2,1,0:T(8,128)} %param.7) | copy-start | bytes 786436
  2.7 16.4 %copy-start.4 = (f32[32,128]{1,0:T(8,128)S(1)}, f32[32,128]{1,0:T(8,128)}, u32[]{:S(2)}) copy-start(f32[32,128]{1,0:T(8,128)} %surface.3) | copy-start | bytes 49156
  2.7 24.4 %all-to-all-start = ((bf16[8,80,128]{2,1,0:T(8,128)(2,1)}), bf16[8,80,128]{2,1,0:T(8,128)(2,1)S(1)}, u32[]{:S(2)}, u32[]{:S(2)}) async-start(bf16[8,80,128]{2,1,0:T(8,128)(2,1)} %shard_map.94), calls=%async_computation | async-start | bytes 327680 | tf_op jit(solution)/shard_map/all_to_all | solution.py:377
  19.1 8.0 %copy-start.3 = (bf16[4,128,128]{2,1,0:T(8,128)(2,1)S(1)}, bf16[4,128,128]{2,1,0:T(8,128)(2,1)}, u32[]{:S(2)}) copy-start(bf16[4,128,128]{2,1,0:T(8,128)(2,1)} %weights.1) | copy-start | bytes 393220
  19.1 8.0 %copy-start.5 = (s32[32,128]{1,0:T(8,128)S(1)}, s32[32,128]{1,0:T(8,128)}, u32[]{:S(2)}) copy-start(s32[32,128]{1,0:T(8,128)} %trigger.1) | copy-start | bytes 49156
  19.1 8.0 %copy-start.6 = (s32[32,128]{1,0:T(8,128)S(1)}, s32[32,128]{1,0:T(8,128)}, u32[]{:S(2)}) copy-start(s32[32,128]{1,0:T(8,128)} %closure.1) | copy-start | bytes 49156
  19.5 3.1 %collective-permute-start = (f32[72,128]{1,0:T(8,128)S(1)}, f32[72,128]{1,0:T(8,128)S(1)}, u32[]{:S(2)}, u32[]{:S(2)}) collective-permute-start(f32[72,128]{1,0:T(8,128)S(1)} %get-tuple-element.20), channel_id=1, source_target_pairs={{0,8},{16,24},{32,40},{48,56},{64,72},{80,88},{96,104},{112,120},{... | collective-permute-start | bytes 110600 | tf_op jit(solution)/shard_map/ppermute | solution.py:384
  28.2 15.0 %all-to-all-start.1 = ((bf16[8,88,128]{2,1,0:T(8,128)(2,1)}), bf16[8,88,128]{2,1,0:T(8,128)(2,1)S(1)}, u32[]{:S(2)}, u32[]{:S(2)}) async-start(bf16[8,88,128]{2,1,0:T(8,128)(2,1)} %get-tuple-element.23), calls=%async_computation.1 | async-start | bytes 360448 | tf_op jit(solution)/shard_map/all_to_all | solution.py:394
  32.9 11.5 %collective-permute-start.1 = (f32[64,128]{1,0:T(8,128)S(1)}, f32[64,128]{1,0:T(8,128)S(1)}, u32[]{:S(2)}, u32[]{:S(2)}) collective-permute-start(f32[64,128]{1,0:T(8,128)S(1)} %get-tuple-element.22), channel_id=1, source_target_pairs={{8,16},{24,32},{40,48},{56,64},{72,80},{88,96},{104,112},{120,128}... | collective-permute-start | bytes 98312 | tf_op jit(solution)/shard_map/ppermute | solution.py:395

commit v6 on v5

--- a/solution.py
+++ b/solution.py
@@ -335,18 +335,15 @@
     put_halos(chip_w, from_chip[32:64, :], right, edge_w, None)
     evolve(edge_p, edge_w)
     fixed = edge_lanes(right)
-    for first in range(0, OWN, 4):
-        for level in range(first, first + 4):
+    for index, (edge, local, done, out) in enumerate(
+        ((edge_p, local_p, done_p, out_p), (edge_w, local_w, done_w, out_w))
+    ):
+        for level in range(OWN):
             at = pl.ds(level * ROWS, ROWS)
-            done_p[at, :] = jnp.where(fixed, edge_of(edge_p, level, right), local_p[at, :])
-            done_w[at, :] = jnp.where(fixed, edge_of(edge_w, level, right), local_w[at, :])
-        block = pl.ds(first * ROWS, 4 * ROWS)
-        for index, (done, out) in enumerate(((done_p, out_p), (done_w, out_w))):
-            copy = pltpu.make_async_copy(
-                done.at[block, :], out.at[block, :], sems.at[4 * index + first // 4]
-            )
-            copy.start()
-            copies.append(copy)
+            done[at, :] = jnp.where(fixed, edge_of(edge, level, right), local[at, :])
+        copy = pltpu.make_async_copy(done, out, sems.at[index])
+        copy.start()
+        copies.append(copy)
     for copy in copies:
         copy.wait()
 

time: 46.6 us -> 46.6 us (level)
  no operation moved by 1% of the time
where the time goes in v6:
time: 46.6 us; the launch traced here: 46.2 us
  starting transfers between devices  32.1 us (69%)
  Pallas kernels  7.77 us (17%)
  waiting for transfers between devices  5.63 us (12%)
  between operations  0.75 us (2%)
    all_to_all x1, starting transfers between devices, coupled(): columns = lax.all_to_all(columns, 'lev', 0, 0, tiled=True)  16.4 us
    ppermute x1, starting transfers between devices, coupled(): lax.ppermute(to_chip, 'tile', between + [(b, a) for a, b in between])  9.03 us
    all_to_all x1, starting transfers between devices, coupled(): heats = lax.all_to_all(heats, 'lev', 0, 0, tiled=True)  4.75 us
    all_to_all x1, waiting for transfers between devices, coupled(): columns = lax.all_to_all(columns, 'lev', 0, 0, tiled=True)  4.44 us
    pallas_call x1, Pallas kernels, coupled(): call(send_columns, [((PEERS, 80, LANES), BF16)], room=60 << 20)  2.05 us
    ppermute x1, starting transfers between devices, coupled(): lax.ppermute(to_core, 'tile', within + [(b, a) for a, b in within])  1.92 us
    pallas_call x1, Pallas kernels, coupled(): call(finish, [(flat, F32), (flat, F32), (flat, BF16)], [(packed, F32)] *...  1.77 us
    pallas_call x1, Pallas kernels, coupled(): call(local_substeps, [(flat, F32)] * 2 + [(packed, F32)] * 4, flops=20000...  1.24 us
  transfers between devices with their start and end apart: 4, of which 2 were waited for; matrix products, arithmetic and copies ran while one was open for 0% of the time, Pallas kernels for 6%

profile of v6, /device:TPU:16, one launch (start us, length us, event | category | flops | bytes accessed | tf_op | source)
XLA Modules:
  0.0 46.2 jit_solution(2607699745399860776)
XLA Ops:
  0.6 0.0 copy-start.1
  0.6 0.0 copy-start.2
  0.7 2.1 %shard_map.94 = bf16[8,80,128]{2,1,0:T(8,128)(2,1)} custom-call(f32[512,128]{1,0:T(8,128)} %bitcast.6, f32[512,128]{1,0:T(8,128)} %bitcast.9), custom_call_target="tpu_custom_call" | custom-call | flops 100000 | bytes 1000000 | tf_op jit(solution)/shard_map/pallas_call | solution.py:371
  2.7 0.0 copy-start
  2.7 0.0 copy-start.4
  2.7 16.4 %all-to-all-start = ((bf16[8,80,128]{2,1,0:T(8,128)(2,1)}), bf16[8,80,128]{2,1,0:T(8,128)(2,1)S(1)}, u32[]{:S(2)}, u32[]{:S(2)}) async-start(bf16[8,80,128]{2,1,0:T(8,128)(2,1)} %shard_map.94), calls=%async_computation | async-start | bytes 327680 | tf_op jit(solution)/shard_map/all_to_all | solution.py:374
  19.1 0.0 copy-done.1
  19.1 0.0 copy-done.2
  19.1 0.0 copy-done
  19.1 0.0 copy-done.4
  19.1 0.0 copy-start.3
  19.1 0.0 copy-start.5
  19.1 0.0 copy-start.6
  19.1 0.4 shard_map.95
  19.5 1.9 %collective-permute-start = (f32[72,128]{1,0:T(8,128)S(1)}, f32[72,128]{1,0:T(8,128)S(1)}, u32[]{:S(2)}, u32[]{:S(2)}) collective-permute-start(f32[72,128]{1,0:T(8,128)S(1)} %get-tuple-element.20), channel_id=1, source_target_pairs={{0,8},{16,24},{32,40},{48,56},{64,72},{80,88},{96,104},{112,120},{... | collective-permute-start | bytes 110600 | tf_op jit(solution)/shard_map/ppermute | solution.py:381
  21.5 1.2 %collective-permute-done.from_core = f32[72,128]{1,0:T(8,128)S(1)} collective-permute-done((f32[72,128]{1,0:T(8,128)S(1)}, f32[72,128]{1,0:T(8,128)S(1)}, u32[]{:S(2)}, u32[]{:S(2)}) %collective-permute-start) | collective-permute-done | bytes 36896 | tf_op jit(solution)/shard_map/ppermute | solution.py:381
  22.6 4.4 %all-to-all-done.got = bf16[8,80,128]{2,1,0:T(8,128)(2,1)S(1)} async-done(((bf16[8,80,128]{2,1,0:T(8,128)(2,1)}), bf16[8,80,128]{2,1,0:T(8,128)(2,1)S(1)}, u32[]{:S(2)}, u32[]{:S(2)}) %all-to-all-start) | async-done | bytes 163872 | tf_op jit(solution)/shard_map/all_to_all | solution.py:374
  27.1 0.0 copy-done.3
  27.1 0.0 copy-done.5
  27.1 0.0 copy-done.6
  27.1 1.1 %shard_map.96 = (bf16[8,88,128]{2,1,0:T(8,128)(2,1)}, f32[64,128]{1,0:T(8,128)S(1)}) custom-call(bf16[8,80,128]{2,1,0:T(8,128)(2,1)S(1)} %all-to-all-done.got, s32[32,128]{1,0:T(8,128)S(1)} %copy-done.5, s32[32,128]{1,0:T(8,128)S(1)} %copy-done.6, bf16[4,128,128]{2,1,0:T(8,128)(2,1)S(1)} %copy-done.3, f32[72,128]{1,0:T(8,128)S(1)} %collective-permute-done.from_core, ...), custom_call_target="tpu_custom_call" | custom-call | flops 70000000 | bytes 1000000 | tf_op jit(solution)/shard_map/pallas_call | solution.py:385
  28.2 4.7 %all-to-all-start.1 = ((bf16[8,88,128]{2,1,0:T(8,128)(2,1)}), bf16[8,88,128]{2,1,0:T(8,128)(2,1)S(1)}, u32[]{:S(2)}, u32[]{:S(2)}) async-start(bf16[8,88,128]{2,1,0:T(8,128)(2,1)} %get-tuple-element.23), calls=%async_computation.1 | async-start | bytes 360448 | tf_op jit(solution)/shard_map/all_to_all | solution.py:391
  32.9 9.0 %collective-permute-start.1 = (f32[64,128]{1,0:T(8,128)S(1)}, f32[64,128]{1,0:T(8,128)S(1)}, u32[]{:S(2)}, u32[]{:S(2)}) collective-permute-start(f32[64,128]{1,0:T(8,128)S(1)} %get-tuple-element.22), channel_id=1, source_target_pairs={{8,16},{24,32},{40,48},{56,64},{72,80},{88,96},{104,112},{120,128}... | collective-permute-start | bytes 98312 | tf_op jit(solution)/shard_map/ppermute | solution.py:392
  42.0 1.2 %shard_map.97 = (f32[512,128]{1,0:T(8,128)S(1)}, f32[512,128]{1,0:T(8,128)S(1)}, f32[128,128]{1,0:T(8,128)S(1)}, f32[128,128]{1,0:T(8,128)S(1)}, f32[128,128]{1,0:T(8,128)S(1)}, /*index=5*/f32[128,128]{1,0:T(8,128)S(1)}) custom-call(f32[512,128]{1,0:T(8,128)S(1)} %bitcast.8, f32[512,128]{1,0:T(8,128)S(1)} %bitcast.11, f32[512,128]{1,0:T(8,128)S(1)} %bitcast.13, ...), custom_call_target="tpu_custom_call" | custom-call | flops 20000000 | bytes 1000000 | tf_op jit(solution)/shard_map/pallas_call | solution.py:382
  43.2 0.0 all-to-all-done.1.got
  43.2 1.2 %shard_map.98 = (bf16[512,128]{1,0:T(8,128)(2,1)S(1)}, f32[512,128]{1,0:T(8,128)S(1)}, f32[512,128]{1,0:T(8,128)S(1)}, f32[128,128]{1,0:T(8,128)S(1)}) custom-call(bf16[8,88,128]{2,1,0:T(8,128)(2,1)S(1)} %all-to-all-done.1.got, f32[72,128]{1,0:T(8,128)S(1)} %collective-permute-done.from_core, f32[512,128]{1,0:T(8,128)S(1)} %get-tuple-element.24.local_p, ...), custom_call_target="tpu_custom_call" | custom-call | flops 100000 | bytes 1000000 | tf_op jit(solution)/shard_map/pallas_call | solution.py:393
  44.5 0.0 collective-permute-done.1.from_chip
  44.5 1.8 %shard_map.99 = (f32[512,128]{1,0:T(8,128)}, f32[512,128]{1,0:T(8,128)}, bf16[512,128]{1,0:T(8,128)(2,1)}) custom-call(f32[64,128]{1,0:T(8,128)S(1)} %collective-permute-done.1.from_chip, bf16[512,128]{1,0:T(8,128)(2,1)S(1)} %get-tuple-element.29.heating, f32[512,128]{1,0:T(8,128)S(1)} %get-tuple-element.30.local_p, ...), custom_call_target="tpu_custom_call" | custom-call | flops 100000 | bytes 1000000 | tf_op jit(solution)/shard_map/pallas_call | solution.py:398
Async XLA Ops:
  0.6 18.5 %copy-start.1 = (f32[16,32,128]{2,1,0:T(8,128)S(1)}, f32[16,32,128]{2,1,0:T(8,128)}, u32[]{:S(2)}) copy-start(f32[16,32,128]{2,1,0:T(8,128)} %param.8) | copy-start | bytes 786436
  0.6 18.4 %copy-start.2 = (f32[16,32,128]{2,1,0:T(8,128)S(1)}, f32[16,32,128]{2,1,0:T(8,128)}, u32[]{:S(2)}) copy-start(f32[16,32,128]{2,1,0:T(8,128)} %param.9) | copy-start | bytes 786436
  2.7 16.4 %copy-start = (f32[16,32,128]{2,1,0:T(8,128)S(1)}, f32[16,32,128]{2,1,0:T(8,128)}, u32[]{:S(2)}) copy-start(f32[16,32,128]{2,1,0:T(8,128)} %param.7) | copy-start | bytes 786436
  2.7 16.4 %copy-start.4 = (f32[32,128]{1,0:T(8,128)S(1)}, f32[32,128]{1,0:T(8,128)}, u32[]{:S(2)}) copy-start(f32[32,128]{1,0:T(8,128)} %surface.3) | copy-start | bytes 49156
  2.7 24.4 %all-to-all-start = ((bf16[8,80,128]{2,1,0:T(8,128)(2,1)}), bf16[8,80,128]{2,1,0:T(8,128)(2,1)S(1)}, u32[]{:S(2)}, u32[]{:S(2)}) async-start(bf16[8,80,128]{2,1,0:T(8,128)(2,1)} %shard_map.94), calls=%async_computation | async-start | bytes 327680 | tf_op jit(solution)/shard_map/all_to_all | solution.py:374
  19.1 8.0 %copy-start.3 = (bf16[4,128,128]{2,1,0:T(8,128)(2,1)S(1)}, bf16[4,128,128]{2,1,0:T(8,128)(2,1)}, u32[]{:S(2)}) copy-start(bf16[4,128,128]{2,1,0:T(8,128)(2,1)} %weights.1) | copy-start | bytes 393220
  19.1 8.0 %copy-start.5 = (s32[32,128]{1,0:T(8,128)S(1)}, s32[32,128]{1,0:T(8,128)}, u32[]{:S(2)}) copy-start(s32[32,128]{1,0:T(8,128)} %trigger.1) | copy-start | bytes 49156
  19.1 8.0 %copy-start.6 = (s32[32,128]{1,0:T(8,128)S(1)}, s32[32,128]{1,0:T(8,128)}, u32[]{:S(2)}) copy-start(s32[32,128]{1,0:T(8,128)} %closure.1) | copy-start | bytes 49156
  19.5 3.1 %collective-permute-start = (f32[72,128]{1,0:T(8,128)S(1)}, f32[72,128]{1,0:T(8,128)S(1)}, u32[]{:S(2)}, u32[]{:S(2)}) collective-permute-start(f32[72,128]{1,0:T(8,128)S(1)} %get-tuple-element.20), channel_id=1, source_target_pairs={{0,8},{16,24},{32,40},{48,56},{64,72},{80,88},{96,104},{112,120},{... | collective-permute-start | bytes 110600 | tf_op jit(solution)/shard_map/ppermute | solution.py:381
  28.2 15.0 %all-to-all-start.1 = ((bf16[8,88,128]{2,1,0:T(8,128)(2,1)}), bf16[8,88,128]{2,1,0:T(8,128)(2,1)S(1)}, u32[]{:S(2)}, u32[]{:S(2)}) async-start(bf16[8,88,128]{2,1,0:T(8,128)(2,1)} %get-tuple-element.23), calls=%async_computation.1 | async-start | bytes 360448 | tf_op jit(solution)/shard_map/all_to_all | solution.py:391
  32.9 11.5 %collective-permute-start.1 = (f32[64,128]{1,0:T(8,128)S(1)}, f32[64,128]{1,0:T(8,128)S(1)}, u32[]{:S(2)}, u32[]{:S(2)}) collective-permute-start(f32[64,128]{1,0:T(8,128)S(1)} %get-tuple-element.22), channel_id=1, source_target_pairs={{8,16},{24,32},{40,48},{56,64},{72,80},{88,96},{104,112},{120,128}... | collective-permute-start | bytes 98312 | tf_op jit(solution)/shard_map/ppermute | solution.py:392
